TPU v7x, 32 devices: a whole 2x2x4 slice. The times are simulated.
32 devices in a mesh: group: 4 (over y, x), shard: 8 (over z, core).
Axes of the slice: x: 2, y: 2, z: 4, core: 2. Of those that a mesh axis runs over, the one named last changes fastest.
Arguments:
- queries: float32 [256, 768], P(('group', 'shard')), may hold values from -6 to 6
- codebook: float32 [96, 256, 8], replicated, may hold values from -0.21875 to 0.21875
- pq_codes: int32 [256, 96, 256], P(('group', 'shard')), may hold values from 0 to 255
- probes: int32 [256, 8], P('group'), may hold values from 0 to 63, all different within a row
- vectors: float32 [32768, 768], P(('group', 'shard')), may hold values from -0.21875 to 0.21875
- cand_owner: int32 [256, 16], P(('group', 'shard')), may hold values from 0 to 31, all different within a row; in each aligned block of 8 rows (0 to 7, 8 to 15, ...) at most 4 rows name the same one
- cand_row: int32 [256, 16], P(('group', 'shard')), may hold values from 0 to 1023
Outputs:
- pq_scores: float32 [256, 256, 64], P(('group', 'shard'))
- rerank_scores: float32 [256, 16], P(('group', 'shard'))
Inputs may be any that keep to these rules, and one draw needn't show every extreme that they name: The 8 probes of one query are distinct. `cand_owner`: the 16 owners of one query are distinct. Among the queries of one device no owner appears more than 4 times, and some owner appears exactly 4 times.
All inputs are finite; a program needn't handle non-finite values.
Results may differ from a plain program's by a relative error of at most 0.0029.
Values may be sent and summed in bfloat16 or wider, within the bound.
No kernel may reach another device: no remote copies, remote signals or barrier semaphores. Data moves between devices by JAX's collectives and lax.ppermute only.
A program may use at most 128 MiB of HBM per device.

v0:
```python
import jax
import jax.numpy as jnp
from jax import lax
from jax.experimental import pallas as pl
from jax.experimental.pallas import tpu as pltpu
from jax.sharding import PartitionSpec as P


AXES = ("group", "shard")
SUB = 8
LANE = 128
GATHER = lax.GatherDimensionNumbers(
    offset_dims=(),
    collapsed_slice_dims=(1,),
    start_index_map=(1,),
    operand_batching_dims=(0,),
    start_indices_batching_dims=(0,),
)


def pick(table, index):
    return lax.gather(
        table, index[..., None], GATHER, (1, 1), mode=lax.GatherScatterMode.PROMISE_IN_BOUNDS
    )


def pick_wide(table, index):
    low = jnp.bitwise_and(index, LANE - 1)
    result = pick(table[:, :LANE], low)
    for part in range(1, table.shape[1] // LANE):
        found = pick(table[:, part * LANE : (part + 1) * LANE], low)
        result = jnp.where(index >= part * LANE, found, result)
    return result


def split3(x):
    high = x.astype(jnp.bfloat16)
    rest = x - high.astype(jnp.float32)
    middle = rest.astype(jnp.bfloat16)
    low = (rest - middle.astype(jnp.float32)).astype(jnp.bfloat16)
    return high, middle, low


def owner_table(owner, row, owners):
    q_dev, cands = owner.shape
    width = -(-owners // LANE) * LANE
    lane = lax.broadcasted_iota(jnp.int32, (q_dev, width), 1)
    table = jnp.full((q_dev, width), -1, jnp.int32)
    for c in range(cands):
        table = jnp.where(lane == owner[:, c : c + 1], row[:, c : c + 1], table)
    return table


def before(table):
    asked = (table >= 0).astype(jnp.int32)
    rows = [jnp.zeros_like(asked[0:1])]
    for q in range(1, table.shape[0]):
        rows.append(rows[-1] + asked[q - 1 : q])
    return jnp.concatenate(rows, axis=0)


def layout_of(pair_count, owners, width):
    capacity = max(2, pair_count // owners)
    parts = max(
        p for p in range(1, 9) if p == 1 or (p * capacity <= SUB and width % (p * LANE) == 0)
    )
    return capacity, parts


def ids_kernel(capacity, parts, owner_ref, row_ref, out_ref):
    owners = out_ref.shape[0]
    table = owner_table(owner_ref[...], row_ref[...], owners)
    rank = before(table)
    rows = []
    for s in range(capacity):
        rows.append(jnp.max(jnp.where(rank == s, table, -1), axis=0, keepdims=True))
    rows = rows * parts
    rows += [jnp.full_like(rows[0], -1)] * (SUB - len(rows))
    packed = jnp.concatenate(rows, axis=0)
    for block in range(packed.shape[1] // LANE):
        square = jnp.concatenate(
            [packed[:, block * LANE : (block + 1) * LANE]]
            + [jnp.zeros((LANE - SUB, LANE), jnp.int32)],
            axis=0,
        )
        count = min(LANE, owners - block * LANE)
        turned = square.T[:count]
        out_ref[block * LANE : block * LANE + count] = turned.reshape(count, 1, LANE)


def rows_kernel(capacity, parts, ids_ref, vectors_ref, out_ref):
    sources, slots = out_ref.shape[0], out_ref.shape[1]
    count, width = vectors_ref.shape
    piece = width // parts
    shape = (sources, slots, LANE)
    lane = lax.broadcasted_iota(jnp.int32, shape, 2)
    own = jnp.where(lane == lax.broadcasted_iota(jnp.int32, shape, 1), ids_ref[...], 0)
    ids = jnp.sum(own, axis=2, keepdims=True).reshape(sources * slots, 1)
    pieces = []
    for block in range(count // LANE):
        lane = lax.broadcasted_iota(jnp.int32, (sources * slots, LANE), 1) + block * LANE
        pieces.append(jnp.where(ids == lane, 1.0, 0.0).astype(jnp.bfloat16))
    chosen = jnp.concatenate(pieces, axis=1)
    slot = lax.broadcasted_iota(jnp.int32, (sources * slots, piece), 0) % slots
    result = None
    for part in range(parts):
        vectors = vectors_ref[:, part * piece : (part + 1) * piece].astype(jnp.bfloat16)
        found = jnp.dot(chosen, vectors, preferred_element_type=jnp.float32)
        result = found if part == 0 else jnp.where(slot >= part * capacity, found, result)
    out_ref[...] = result.reshape(sources, slots, piece).astype(jnp.bfloat16)


def final_kernel(capacity, parts, owner_ref, row_ref, queries_ref, rows_ref, out_ref):
    owners, slots, piece = rows_ref.shape
    q_dev, cands = out_ref.shape
    rows = rows_ref[...].reshape(owners * slots, piece)
    total = None
    for part in range(parts):
        x = queries_ref[:, part * piece : (part + 1) * piece]
        stacked = jnp.concatenate(split3(x), axis=0)
        product = lax.dot_general(
            stacked, rows, (((1,), (1,)), ((), ())), preferred_element_type=jnp.float32
        )
        scores = product[:q_dev] + product[q_dev : 2 * q_dev] + product[2 * q_dev :]
        if part:
            width = scores.shape[1]
            scores = pltpu.roll(scores, width - part * capacity, axis=1)
        total = scores if part == 0 else total + scores
    owner = owner_ref[...]
    padded = jnp.concatenate([owner, jnp.zeros((q_dev, LANE - cands), jnp.int32)], axis=1)
    rank = before(owner_table(owner, row_ref[...], owners))
    place = padded * slots + pick_wide(rank, padded)
    out_ref[...] = pick_wide(total, place)[:, :cands]


def join_kernel(*refs):
    rows = refs[0].shape[0]
    for n, ref in enumerate(refs[:-1]):
        refs[-1][n * rows : (n + 1) * rows] = ref[...]


def lists_kernel(lists, probes_ref, out_ref):
    total = probes_ref.shape[1]
    width = out_ref.shape[1]
    shard = lax.axis_index("shard")
    wanted = shard * lists + lax.broadcasted_iota(jnp.int32, (lists, total), 0)
    hit = jnp.zeros((lists, total), jnp.int32)
    for p in range(probes_ref.shape[0]):
        hit = jnp.where(probes_ref[p : p + 1, :] == wanted, 1, hit)
    upto = lax.broadcasted_iota(jnp.int32, (total, total), 0) >= lax.broadcasted_iota(
        jnp.int32, (total, total), 1
    )
    running = lax.dot_general(
        upto.astype(jnp.float32).astype(jnp.bfloat16),
        hit.astype(jnp.float32).astype(jnp.bfloat16),
        (((1,), (1,)), ((), ())),
        preferred_element_type=jnp.float32,
    )
    rank = lax.broadcasted_iota(jnp.int32, (total, width), 1).astype(jnp.float32)
    position = lax.broadcasted_iota(jnp.int32, (lists, total), 1)
    last = jnp.max(jnp.where(hit > 0, position, 0), axis=1, keepdims=True)
    counts = jnp.sum(hit, axis=1, keepdims=True)
    found = []
    for n in range(lists):
        passed = jnp.where(running[:, n : n + 1] <= rank, 1.0, 0.0)
        found.append(jnp.sum(passed, axis=0, keepdims=True))
    found = jnp.concatenate(found, axis=0).astype(jnp.int32)
    place = lax.broadcasted_iota(jnp.int32, (lists, width), 1)
    found = jnp.where(place < counts, found, last)
    found = jnp.where(place == width - 1, counts, found)
    out_ref[...] = found


def pq_kernel(q_dev, pieces, unroll, lists_hbm, codebook_ref, wide_codes, *refs):
    number = len(pieces)
    chunk_refs, (out_ref, queries, table, codes, lists_s, sems) = (
        refs[:number],
        refs[number:],
    )
    lists, subs, entries = codes.shape
    total = queries.shape[0]
    centres = codebook_ref.shape[1]
    rows = 2 * SUB
    blocks = subs // rows
    shard = lax.axis_index("shard")

    send = pltpu.make_async_copy(lists_hbm, lists_s, sems.at[1])
    send.start()

    for (offset, begin, size), ref in zip(pieces, chunk_refs):
        start = 0 if offset is None else jnp.bitwise_xor(shard, offset) * q_dev
        queries[pl.ds(pl.multiple_of(start, q_dev), size), :] = ref[begin : begin + size, :]

    out_ref[...] = jnp.zeros(out_ref.shape, jnp.float32)

    half = LANE // 2
    lane = lax.broadcasted_iota(jnp.int32, (total, LANE), 1)
    inside = lax.broadcasted_iota(jnp.int32, (1, SUB, LANE), 2) % half // (half // SUB)
    own = jnp.where(inside == lax.broadcasted_iota(jnp.int32, (1, SUB, LANE), 1), 1.0, 0.0)

    def columns(k, carry):
        x = queries[:, pl.ds(pl.multiple_of(k * LANE, LANE), LANE)]
        swapped = pltpu.roll(x, half, axis=1)
        products = []
        for side in range(2):
            wide = jnp.where((lane < half) == (side == 0), x, swapped)
            high = wide.astype(jnp.bfloat16).astype(jnp.float32)
            terms = []
            for term in (high, wide - high):
                spread = (term[:, None, :] * own).reshape(total * SUB, LANE)
                terms.append(spread.astype(jnp.bfloat16))
            c = codebook_ref[pl.ds(pl.multiple_of(k * LANE + side * half, half), half), :]
            c_high = c.astype(jnp.bfloat16)
            c_low = (c - c_high.astype(jnp.float32)).astype(jnp.bfloat16)
            weights = jnp.concatenate([c_high, c_low, c_high, c_low], axis=0)
            product = jnp.dot(
                jnp.concatenate(terms, axis=1), weights, preferred_element_type=jnp.float32
            )
            products.append(product.reshape(total, SUB, centres))
        table[:, k] = jnp.concatenate(products, axis=1).astype(jnp.bfloat16)
        return carry

    lax.fori_loop(0, blocks, columns, 0)
    for n in range(lists):
        codes[n] = wide_codes[n].astype(jnp.int16)
    send.wait()
    halves = entries // LANE
    width = lists_s.shape[1]

    def emit(n, chosen, sums):
        for u in range(unroll):
            line = [
                jnp.sum(s, axis=0, keepdims=True) for s in sums[u * halves : (u + 1) * halves]
            ]
            out_ref[n, pl.ds(chosen[u], 1), :] = jnp.concatenate(line, axis=1)

    def one_list(n, carry):
        count = lists_s[n, width - 1]

        def some(step, inner):
            chosen = tuple(lists_s[n, step * unroll + u] for u in range(unroll))
            sums = [None] * (unroll * halves)
            for i in range(blocks):
                for h in range(halves):
                    code = codes[n, i * rows : (i + 1) * rows, h * LANE : (h + 1) * LANE]
                    low = jnp.bitwise_and(code, jnp.int16(LANE - 1))
                    for u in range(unroll):
                        value = pick(table[chosen[u], i, :, 0:LANE], low)
                        for part in range(1, centres // LANE):
                            other = pick(
                                table[chosen[u], i, :, part * LANE : (part + 1) * LANE], low
                            )
                            value = jnp.where(code >= jnp.int16(part * LANE), other, value)
                        value = value.astype(jnp.float32)
                        value = value[:SUB] + value[SUB:]
                        at = u * halves + h
                        sums[at] = value if i == 0 else sums[at] + value
                if i == 1:
                    emit(*inner)
            return n, chosen, tuple(sums)

        return lax.fori_loop(0, (count + unroll - 1) // unroll, some, carry)

    first = (
        jnp.int32(0),
        (jnp.int32(0),) * unroll,
        (jnp.zeros((SUB, LANE), jnp.float32),) * (unroll * halves),
    )
    emit(*lax.fori_loop(0, lists, one_list, first))


def whole(memory=pltpu.VMEM):
    return pl.BlockSpec(memory_space=memory)


def per_device(queries, codebook, pq_codes, probes, vectors, cand_owner, cand_row):
    shards = lax.axis_size("shard")
    owners = lax.axis_size("group") * shards
    q_dev, width = queries.shape
    cands = cand_owner.shape[1]
    subs, centres, dims = codebook.shape
    lists, _, entries = pq_codes.shape
    total = q_dev * shards
    capacity, parts = layout_of(q_dev * cands, owners, width)
    unroll = 8

    ids = pl.pallas_call(
        lambda *refs: ids_kernel(capacity, parts, *refs),
        out_shape=jax.ShapeDtypeStruct((owners, 1, LANE), jnp.int32),
        in_specs=[whole()] * 2,
        out_specs=whole(),
        name="ids",
        cost_estimate=pl.CostEstimate(flops=10**9, bytes_accessed=6 << 20, transcendentals=0),
    )(cand_owner, cand_row)
    list_width = -(-(total + unroll + 1) // LANE) * LANE
    grouping = pl.pallas_call(
        lambda *refs: lists_kernel(lists, *refs),
        out_shape=jax.ShapeDtypeStruct((lists, list_width), jnp.int32),
        in_specs=[whole()],
        out_specs=whole(),
        name="groups",
        compiler_params=pltpu.CompilerParams(vmem_limit_bytes=4 << 20),
        cost_estimate=pl.CostEstimate(flops=10**9, bytes_accessed=12 << 20, transcendentals=0),
    )
    groups = grouping(probes.T)
    own, groups = lax.optimization_barrier((queries, groups))
    asked = lax.all_to_all(ids, AXES, split_axis=0, concat_axis=0, tiled=True)

    near = [queries]
    if shards == 8:
        near += [
            lax.ppermute(own, "shard", [(i, i ^ k) for i in range(shards)])
            for k in range(2, shards, 2)
        ]
    else:
        gathered = lax.all_gather(queries, "shard", axis=0, tiled=True)

    rows = pl.pallas_call(
        lambda *refs: rows_kernel(capacity, parts, *refs),
        out_shape=jax.ShapeDtypeStruct((owners, SUB, width // parts), jnp.bfloat16),
        in_specs=[whole()] * 2,
        out_specs=whole(),
        name="rows",
        compiler_params=pltpu.CompilerParams(vmem_limit_bytes=16 << 20),
        cost_estimate=pl.CostEstimate(flops=10**9, bytes_accessed=4 << 20, transcendentals=0),
    )(asked, vectors)
    returned = lax.all_to_all(rows, AXES, split_axis=0, concat_axis=0, tiled=True)
    pieces, chunks = [], []
    if shards == 8:
        joined = pl.pallas_call(
            join_kernel,
            out_shape=jax.ShapeDtypeStruct((len(near) * q_dev, width), jnp.float32),
            in_specs=[whole()] * len(near),
            out_specs=whole(),
            name="join",
            compiler_params=pltpu.CompilerParams(vmem_limit_bytes=4 << 20),
            cost_estimate=pl.CostEstimate(flops=10**9, bytes_accessed=16 << 20, transcendentals=0),
        )(*near)
        other = lax.ppermute(joined, "shard", [(i, i ^ 1) for i in range(shards)])
        for side, chunk in enumerate((joined, other)):
            for n in range(len(near)):
                chunks.append(chunk)
                pieces.append((2 * n ^ side, n * q_dev, q_dev))
    else:
        pieces.append((None, 0, total))
        chunks.append(gathered)

    pq = pl.pallas_call(
        lambda *refs: pq_kernel(q_dev, pieces, unroll, *refs),
        out_shape=jax.ShapeDtypeStruct((lists, total, entries), jnp.float32),
        in_specs=[whole(pl.ANY)] + [whole()] * 2 + [whole()] * len(chunks),
        out_specs=whole(),
        scratch_shapes=[
            pltpu.VMEM((total, width), jnp.float32),
            pltpu.VMEM((total, subs // SUB // 2, 2 * SUB, centres), jnp.bfloat16),
            pltpu.VMEM((lists, subs, entries), jnp.int16),
            pltpu.SMEM((lists, list_width), jnp.int32),
            pltpu.SemaphoreType.DMA((3,)),
        ],
        name="pq",
        compiler_params=pltpu.CompilerParams(
            vmem_limit_bytes=14300000
        ),
        cost_estimate=pl.CostEstimate(
            flops=10**10, bytes_accessed=30 << 20, transcendentals=0
        ),
    )(
        groups,
        codebook.transpose(0, 2, 1).reshape(subs * dims, centres),
        pq_codes,
        *chunks,
    )

    rerank = pl.pallas_call(
        lambda *refs: final_kernel(capacity, parts, *refs),
        out_shape=jax.ShapeDtypeStruct((q_dev, cands), jnp.float32),
        in_specs=[whole()] * 4,
        out_specs=whole(),
        name="final",
        compiler_params=pltpu.CompilerParams(vmem_limit_bytes=8 << 20),
    )(cand_owner, cand_row, queries, returned)
    return pq.transpose(0, 2, 1), rerank


def solution(mesh):
    in_specs = (
        P(AXES, None),
        P(),
        P(AXES, None, None),
        P("group", None),
        P(AXES, None),
        P(AXES, None),
        P(AXES, None),
    )
    out_specs = (P(AXES, None, None), P(AXES, None))
    return jax.shard_map(
        per_device, mesh=mesh, in_specs=in_specs, out_specs=out_specs, check_vma=False
    )
```

profile of v0, /device:TPU:13, one launch (start us, length us, event | category | flops | bytes accessed | tf_op | source)
XLA Modules:
  0.0 38.3 jit_solution(14274772262672498308)
XLA Ops:
  0.6 0.0 copy-start
  0.6 0.0 copy-start.6
  0.6 0.7 %copy-done.6 = s32[64,8]{0,1:T(8,128)S(1)} copy-done((s32[64,8]{0,1:T(8,128)S(1)}, s32[64,8]{0,1:T(8,128)}, u32[]{:S(2)}) %copy-start.6) | copy-done | bytes 2072
  1.3 0.3 groups.1.refs_0_
  1.6 0.0 copy-done
  1.7 0.0 copy-start.3
  1.7 1.4 %collective-permute-start.2 = (f32[8,768]{1,0:T(8,128)S(1)}, f32[8,768]{1,0:T(8,128)S(1)}, u32[]{:S(2)}, u32[]{:S(2)}) collective-permute-start(f32[8,768]{1,0:T(8,128)S(1)} %copy-done), channel_id=1, source_target_pairs={{0,6},{1,7},{2,4},{3,5},{4,2},{5,3},{6,0},{7,1},{8,14},{9,15},{10,... | collective-permute-start | bytes 73736 | tf_op jit(solution)/shard_map/ppermute | solution.py:312
  3.0 1.1 %collective-permute-start.1 = (f32[8,768]{1,0:T(8,128)S(1)}, f32[8,768]{1,0:T(8,128)S(1)}, u32[]{:S(2)}, u32[]{:S(2)}) collective-permute-start(f32[8,768]{1,0:T(8,128)S(1)} %copy-done), channel_id=1, source_target_pairs={{0,4},{1,5},{2,6},{3,7},{4,0},{5,1},{6,2},{7,3},{8,12},{9,13},{10,... | collective-permute-start | bytes 73736 | tf_op jit(solution)/shard_map/ppermute | solution.py:312
  4.1 1.1 %collective-permute-start = (f32[8,768]{1,0:T(8,128)S(1)}, f32[8,768]{1,0:T(8,128)S(1)}, u32[]{:S(2)}, u32[]{:S(2)}) collective-permute-start(f32[8,768]{1,0:T(8,128)S(1)} %copy-done), channel_id=1, source_target_pairs={{0,2},{1,3},{2,0},{3,1},{4,6},{5,7},{6,4},{7,5},{8,10},{9,11},{10,... | collective-permute-start | bytes 73736 | tf_op jit(solution)/shard_map/ppermute | solution.py:312
  5.2 1.5 %ids.1 = s32[32,1,128]{2,1,0:T(1,128)} custom-call(s32[8,16]{1,0:T(8,128)} %refs_0_.5, s32[8,16]{1,0:T(8,128)} %refs_1_.5), custom_call_target="tpu_custom_call" | custom-call | flops 1000000000 | bytes 6291456 | tf_op jit(solution)/shard_map/ids/pallas_call | solution.py:287
  6.8 7.2 %all-to-all-start = ((s32[32,1,128]{2,1,0:T(1,128)}), s32[32,1,128]{2,1,0:T(1,128)S(1)}, u32[]{:S(2)}, u32[]{:S(2)}) async-start(s32[32,1,128]{2,1,0:T(1,128)} %ids.1), calls=%async_computation | async-start | bytes 32768 | tf_op jit(solution)/shard_map/all_to_all | solution.py:307
  13.9 0.0 collective-permute-done.2.refs_3_
  13.9 0.0 collective-permute-done.1.refs_2_
  14.0 0.0 collective-permute-done.refs_1_
  14.0 0.5 %collective-permute-start.3 = (f32[32,768]{1,0:T(8,128)S(1)}, f32[32,768]{1,0:T(8,128)}, u32[]{:S(2)}, u32[]{:S(2)}) collective-permute-start(f32[32,768]{1,0:T(8,128)S(1)} %join.1.refs_3_.refs_4_.refs_5_.refs_6_), channel_id=1, source_target_pairs={{0,1},{1,0},{2,3},{3,2},{4,5},{5,4},{6,7},{7,6},{8,9},{9,8},{10,11... | collective-permute-start | bytes 294920 | tf_op jit(solution)/shard_map/ppermute | solution.py:339
  14.4 4.2 %all-to-all-done.refs_0_ = s32[32,1,128]{2,1,0:T(1,128)S(1)} async-done(((s32[32,1,128]{2,1,0:T(1,128)}), s32[32,1,128]{2,1,0:T(1,128)S(1)}, u32[]{:S(2)}, u32[]{:S(2)}) %all-to-all-start) | async-done | bytes 16416 | tf_op jit(solution)/shard_map/all_to_all | solution.py:307
  18.7 0.0 copy-done.3
  18.7 1.5 %rows.1 = bf16[32,8,384]{2,1,0:T(8,128)(2,1)} custom-call(s32[32,1,128]{2,1,0:T(1,128)S(1)} %all-to-all-done.refs_0_, f32[1024,768]{1,0:T(8,128)S(1)} %copy-done.3), custom_call_target="tpu_custom_call" | custom-call | flops 1000000000 | bytes 4194304 | tf_op jit(solution)/shard_map/rows/pallas_call | solution.py:318
  20.2 4.9 %all-to-all-start.1 = ((bf16[32,8,384]{2,1,0:T(8,128)(2,1)}), bf16[32,8,384]{2,1,0:T(8,128)(2,1)S(1)}, u32[]{:S(2)}, u32[]{:S(2)}) async-start(bf16[32,8,384]{2,1,0:T(8,128)(2,1)} %rows.1), calls=%async_computation.1 | async-start | bytes 393216 | tf_op jit(solution)/shard_map/all_to_all | solution.py:327
  25.1 0.0 collective-permute-done.3.refs_7_.refs_8_.refs_9_.refs_10_
  25.1 0.0 copy-start.4
  25.1 1.1 %copy-done.4 = f32[96,256,8]{1,2,0:T(8,128)S(1)} copy-done((f32[96,256,8]{1,2,0:T(8,128)S(1)}, f32[96,256,8]{1,2,0:T(8,128)}, u32[]{:S(2)}) %copy-start.4) | copy-done | bytes 786456
  26.2 0.0 copy-start.5
  26.2 1.1 %copy-done.5 = s32[8,96,256]{2,1,0:T(8,128)S(1)} copy-done((s32[8,96,256]{2,1,0:T(8,128)S(1)}, s32[8,96,256]{2,1,0:T(8,128)}, u32[]{:S(2)}) %copy-start.5) | copy-done | bytes 786456
  27.4 0.0 copy-start.1
  27.4 0.0 copy-start.2
  27.4 9.9 %pq.1 = f32[8,64,256]{2,1,0:T(8,128)} custom-call(s32[8,128]{1,0:T(8,128)S(1)} %groups.1.refs_0_, f32[768,256]{1,0:T(8,128)S(1)} %bitcast.5, s32[8,96,256]{2,1,0:T(8,128)S(1)} %copy-done.5, f32[32,768]{1,0:T(8,128)S(1)} %join.1.refs_3_.refs_4_.refs_5_.refs_6_, f32[32,768]{1,0:T(8,128)S(1)} %join.1.refs_3_.refs_4_.refs_5_.refs_6_, ...), custom_call_target="tpu_custom_call" | custom-call | flops 10000000000 | bytes 31457280 | tf_op jit(solution)/shard_map/pq/pallas_call | solution.py:348
  37.3 0.0 all-to-all-done.1.refs_3_
  37.3 0.0 copy-done.1
  37.3 0.0 copy-done.2
  37.3 1.0 %final.1 = f32[8,16]{1,0:T(8,128)} custom-call(s32[8,16]{1,0:T(8,128)S(1)} %copy-done.1, s32[8,16]{1,0:T(8,128)S(1)} %copy-done.2, f32[8,768]{1,0:T(8,128)S(1)} %copy-done, bf16[32,8,384]{2,1,0:T(8,128)(2,1)S(1)} %all-to-all-done.1.refs_3_), custom_call_target="tpu_custom_call" | custom-call | tf_op jit(solution)/shard_map/final/pallas_call | solution.py:374
  (1 shorter events, 0.0 us)
Async XLA Ops:
  0.6 1.0 %copy-start = (f32[8,768]{1,0:T(8,128)S(1)}, f32[8,768]{1,0:T(8,128)}, u32[]{:S(2)}) copy-start(f32[8,768]{1,0:T(8,128)} %refs_2_.3) | copy-start | bytes 73732
  0.6 0.7 %copy-start.6 = (s32[64,8]{0,1:T(8,128)S(1)}, s32[64,8]{0,1:T(8,128)}, u32[]{:S(2)}) copy-start(s32[64,8]{0,1:T(8,128)} %param.10) | copy-start | bytes 6148
  1.7 17.0 %copy-start.3 = (f32[1024,768]{1,0:T(8,128)S(1)}, f32[1024,768]{1,0:T(8,128)}, u32[]{:S(2)}) copy-start(f32[1024,768]{1,0:T(8,128)} %refs_1_.4) | copy-start | bytes 9437188
  1.7 12.3 %collective-permute-start.2 = (f32[8,768]{1,0:T(8,128)S(1)}, f32[8,768]{1,0:T(8,128)S(1)}, u32[]{:S(2)}, u32[]{:S(2)}) collective-permute-start(f32[8,768]{1,0:T(8,128)S(1)} %copy-done), channel_id=1, source_target_pairs={{0,6},{1,7},{2,4},{3,5},{4,2},{5,3},{6,0},{7,1},{8,14},{9,15},{10,... | collective-permute-start | bytes 73736 | tf_op jit(solution)/shard_map/ppermute | solution.py:312
  3.0 10.9 %collective-permute-start.1 = (f32[8,768]{1,0:T(8,128)S(1)}, f32[8,768]{1,0:T(8,128)S(1)}, u32[]{:S(2)}, u32[]{:S(2)}) collective-permute-start(f32[8,768]{1,0:T(8,128)S(1)} %copy-done), channel_id=1, source_target_pairs={{0,4},{1,5},{2,6},{3,7},{4,0},{5,1},{6,2},{7,3},{8,12},{9,13},{10,... | collective-permute-start | bytes 73736 | tf_op jit(solution)/shard_map/ppermute | solution.py:312
  4.1 9.8 %collective-permute-start = (f32[8,768]{1,0:T(8,128)S(1)}, f32[8,768]{1,0:T(8,128)S(1)}, u32[]{:S(2)}, u32[]{:S(2)}) collective-permute-start(f32[8,768]{1,0:T(8,128)S(1)} %copy-done), channel_id=1, source_target_pairs={{0,2},{1,3},{2,0},{3,1},{4,6},{5,7},{6,4},{7,5},{8,10},{9,11},{10,... | collective-permute-start | bytes 73736 | tf_op jit(solution)/shard_map/ppermute | solution.py:312
  6.8 11.9 %all-to-all-start = ((s32[32,1,128]{2,1,0:T(1,128)}), s32[32,1,128]{2,1,0:T(1,128)S(1)}, u32[]{:S(2)}, u32[]{:S(2)}) async-start(s32[32,1,128]{2,1,0:T(1,128)} %ids.1), calls=%async_computation | async-start | bytes 32768 | tf_op jit(solution)/shard_map/all_to_all | solution.py:307
  14.0 11.1 %collective-permute-start.3 = (f32[32,768]{1,0:T(8,128)S(1)}, f32[32,768]{1,0:T(8,128)}, u32[]{:S(2)}, u32[]{:S(2)}) collective-permute-start(f32[32,768]{1,0:T(8,128)S(1)} %join.1.refs_3_.refs_4_.refs_5_.refs_6_), channel_id=1, source_target_pairs={{0,1},{1,0},{2,3},{3,2},{4,5},{5,4},{6,7},{7,6},{8,9},{9,8},{10,11... | collective-permute-start | bytes 294920 | tf_op jit(solution)/shard_map/ppermute | solution.py:339
  20.2 17.1 %all-to-all-start.1 = ((bf16[32,8,384]{2,1,0:T(8,128)(2,1)}), bf16[32,8,384]{2,1,0:T(8,128)(2,1)S(1)}, u32[]{:S(2)}, u32[]{:S(2)}) async-start(bf16[32,8,384]{2,1,0:T(8,128)(2,1)} %rows.1), calls=%async_computation.1 | async-start | bytes 393216 | tf_op jit(solution)/shard_map/all_to_all | solution.py:327
  25.1 1.1 %copy-start.4 = (f32[96,256,8]{1,2,0:T(8,128)S(1)}, f32[96,256,8]{1,2,0:T(8,128)}, u32[]{:S(2)}) copy-start(f32[96,256,8]{1,2,0:T(8,128)} %param.8) | copy-start | bytes 2359300
  26.2 1.1 %copy-start.5 = (s32[8,96,256]{2,1,0:T(8,128)S(1)}, s32[8,96,256]{2,1,0:T(8,128)}, u32[]{:S(2)}) copy-start(s32[8,96,256]{2,1,0:T(8,128)} %refs_2_.2) | copy-start | bytes 2359300
  27.4 9.9 %copy-start.1 = (s32[8,16]{1,0:T(8,128)S(1)}, s32[8,16]{1,0:T(8,128)}, u32[]{:S(2)}) copy-start(s32[8,16]{1,0:T(8,128)} %refs_0_.5) | copy-start | bytes 1540
  27.4 9.9 %copy-start.2 = (s32[8,16]{1,0:T(8,128)S(1)}, s32[8,16]{1,0:T(8,128)}, u32[]{:S(2)}) copy-start(s32[8,16]{1,0:T(8,128)} %refs_1_.5) | copy-start | bytes 1540
where the time goes:
time: 38.7 us; the launch traced here: 38.3 us
  starting transfers between devices  16.1 us (42%)
  Pallas kernels  14.2 us (37%)
  waiting for transfers between devices  4.25 us (11%)
  local copies, waits for them, and re-layouts  2.96 us (8%)
  between operations  0.77 us (2%)
    pallas_call x1, Pallas kernels, per_device(): pl.pallas_call(lambda *refs: pq_kernel(q_dev, pieces, unroll, *refs), out...  9.89 us
    all_to_all x1, starting transfers between devices, per_device(): asked = lax.all_to_all(ids, AXES, split_axis=0, concat_axis=0, tiled=True)  7.16 us
    all_to_all x1, starting transfers between devices, per_device(): lax.all_to_all(rows, AXES, split_axis=0, concat_axis=0, tiled=True)  4.88 us
    all_to_all x1, waiting for transfers between devices, per_device(): asked = lax.all_to_all(ids, AXES, split_axis=0, concat_axis=0, tiled=True)  4.24 us
    ppermute x3, starting transfers between devices, per_device(): lax.ppermute(own, 'shard', [(i, i ^ k) for i in range(shards)])  3.56 us
    unnamed x14, local copies, waits for them, and re-layouts  2.96 us
    pallas_call x1, Pallas kernels, per_device(): pl.pallas_call(lambda *refs: rows_kernel(capacity, parts, *refs), out_sha...  1.53 us
    pallas_call x1, Pallas kernels, per_device(): pl.pallas_call(lambda *refs: ids_kernel(capacity, parts, *refs), out_shap...  1.53 us
  transfers between devices with their start and end apart: 6, of which 1 were waited for; matrix products, arithmetic and copies ran while one was open for 0% of the time, Pallas kernels for 34%

commit v1 on v0

--- a/solution.py
+++ b/solution.py
@@ -88,7 +88,38 @@
         out_ref[block * LANE : block * LANE + count] = turned.reshape(count, 1, LANE)
 
 
+def paired_rows_kernel(ids_ref, vectors_ref, out_ref):
+    sources, slots, piece = out_ref.shape
+    count = vectors_ref.shape[0]
+    pairs = sources // 2
+    shape = (pairs, SUB, LANE)
+    lane = lax.broadcasted_iota(jnp.int32, shape, 2)
+    row = lax.broadcasted_iota(jnp.int32, shape, 1)
+    ids = ids_ref[...].reshape(pairs, 2, 1, LANE)
+    mine = jnp.where(row < SUB // 2, ids[:, 0], ids[:, 1])
+    mine = jnp.where(lane == row % (SUB // 2), mine, 0)
+    wanted = jnp.sum(mine, axis=2, keepdims=True).reshape(pairs * SUB, 1)
+    chosen = []
+    for block in range(count // LANE):
+        lane = lax.broadcasted_iota(jnp.int32, (pairs * SUB, LANE), 1) + block * LANE
+        chosen.append(jnp.where(wanted == lane, 1.0, 0.0).astype(jnp.bfloat16))
+    chosen = jnp.concatenate(chosen, axis=1)
+    found = []
+    for part in range(2):
+        vectors = vectors_ref[:, part * piece : (part + 1) * piece].astype(jnp.bfloat16)
+        product = jnp.dot(chosen, vectors, preferred_element_type=jnp.float32)
+        found.append(product.reshape(pairs, SUB, piece))
+    swapped = [pltpu.roll(x, SUB // 2, axis=1) for x in found]
+    upper = lax.broadcasted_iota(jnp.int32, (pairs, SUB, piece), 1) < SUB // 2
+    even = jnp.where(upper, found[0], swapped[1])
+    odd = jnp.where(upper, swapped[0], found[1])
+    result = jnp.stack([even, odd], axis=1).reshape(sources, slots, piece)
+    out_ref[...] = result.astype(jnp.bfloat16)
+
+
 def rows_kernel(capacity, parts, ids_ref, vectors_ref, out_ref):
+    if capacity * 2 == SUB and parts == 2 and out_ref.shape[0] % 2 == 0:
+        return paired_rows_kernel(ids_ref, vectors_ref, out_ref)
     sources, slots = out_ref.shape[0], out_ref.shape[1]
     count, width = vectors_ref.shape
     piece = width // parts

time: 38.7 us -> 38.4 us (level)
  transfers between devices with their start and end apart: 6 -> 6, of which waited for: 1 -> 1; matrix products, arithmetic and copies ran while one was open for 0% -> 0% of each run, Pallas kernels for 34% -> 33%
where the time goes in v1:
time: 38.4 us; the launch traced here: 38 us
  starting transfers between devices  16.1 us (42%)
  Pallas kernels  13.9 us (36%)
  waiting for transfers between devices  4.25 us (11%)
  local copies, waits for them, and re-layouts  2.96 us (8%)
  between operations  0.77 us (2%)
    pallas_call x1, Pallas kernels, per_device(): pl.pallas_call(lambda *refs: pq_kernel(q_dev, pieces, unroll, *refs), out...  9.89 us
    all_to_all x1, starting transfers between devices, per_device(): asked = lax.all_to_all(ids, AXES, split_axis=0, concat_axis=0, tiled=True)  7.16 us
    all_to_all x1, starting transfers between devices, per_device(): lax.all_to_all(rows, AXES, split_axis=0, concat_axis=0, tiled=True)  4.88 us
    all_to_all x1, waiting for transfers between devices, per_device(): asked = lax.all_to_all(ids, AXES, split_axis=0, concat_axis=0, tiled=True)  4.24 us
    ppermute x3, starting transfers between devices, per_device(): lax.ppermute(own, 'shard', [(i, i ^ k) for i in range(shards)])  3.56 us
    unnamed x14, local copies, waits for them, and re-layouts  2.96 us
    pallas_call x1, Pallas kernels, per_device(): pl.pallas_call(lambda *refs: ids_kernel(capacity, parts, *refs), out_shap...  1.53 us
    pallas_call x1, Pallas kernels, per_device(): pl.pallas_call(lambda *refs: rows_kernel(capacity, parts, *refs), out_sha...  1.2 us
  transfers between devices with their start and end apart: 6, of which 1 were waited for; matrix products, arithmetic and copies ran while one was open for 0% of the time, Pallas kernels for 33%

profile of v1, /device:TPU:13, one launch (start us, length us, event | category | flops | bytes accessed | tf_op | source)
XLA Modules:
  0.0 38.0 jit_solution(15164146250150028243)
XLA Ops:
  0.6 0.0 copy-start
  0.6 0.0 copy-start.6
  0.6 0.7 %copy-done.6 = s32[64,8]{0,1:T(8,128)S(1)} copy-done((s32[64,8]{0,1:T(8,128)S(1)}, s32[64,8]{0,1:T(8,128)}, u32[]{:S(2)}) %copy-start.6) | copy-done | bytes 2072
  1.3 0.3 groups.1.refs_0_
  1.6 0.0 copy-done
  1.7 0.0 copy-start.3
  1.7 1.4 %collective-permute-start.2 = (f32[8,768]{1,0:T(8,128)S(1)}, f32[8,768]{1,0:T(8,128)S(1)}, u32[]{:S(2)}, u32[]{:S(2)}) collective-permute-start(f32[8,768]{1,0:T(8,128)S(1)} %copy-done), channel_id=1, source_target_pairs={{0,6},{1,7},{2,4},{3,5},{4,2},{5,3},{6,0},{7,1},{8,14},{9,15},{10,... | collective-permute-start | bytes 73736 | tf_op jit(solution)/shard_map/ppermute | solution.py:343
  3.0 1.1 %collective-permute-start.1 = (f32[8,768]{1,0:T(8,128)S(1)}, f32[8,768]{1,0:T(8,128)S(1)}, u32[]{:S(2)}, u32[]{:S(2)}) collective-permute-start(f32[8,768]{1,0:T(8,128)S(1)} %copy-done), channel_id=1, source_target_pairs={{0,4},{1,5},{2,6},{3,7},{4,0},{5,1},{6,2},{7,3},{8,12},{9,13},{10,... | collective-permute-start | bytes 73736 | tf_op jit(solution)/shard_map/ppermute | solution.py:343
  4.1 1.1 %collective-permute-start = (f32[8,768]{1,0:T(8,128)S(1)}, f32[8,768]{1,0:T(8,128)S(1)}, u32[]{:S(2)}, u32[]{:S(2)}) collective-permute-start(f32[8,768]{1,0:T(8,128)S(1)} %copy-done), channel_id=1, source_target_pairs={{0,2},{1,3},{2,0},{3,1},{4,6},{5,7},{6,4},{7,5},{8,10},{9,11},{10,... | collective-permute-start | bytes 73736 | tf_op jit(solution)/shard_map/ppermute | solution.py:343
  5.2 1.5 %ids.1 = s32[32,1,128]{2,1,0:T(1,128)} custom-call(s32[8,16]{1,0:T(8,128)} %refs_0_.5, s32[8,16]{1,0:T(8,128)} %refs_1_.5), custom_call_target="tpu_custom_call" | custom-call | flops 1000000000 | bytes 6291456 | tf_op jit(solution)/shard_map/ids/pallas_call | solution.py:318
  6.8 7.2 %all-to-all-start = ((s32[32,1,128]{2,1,0:T(1,128)}), s32[32,1,128]{2,1,0:T(1,128)S(1)}, u32[]{:S(2)}, u32[]{:S(2)}) async-start(s32[32,1,128]{2,1,0:T(1,128)} %ids.1), calls=%async_computation | async-start | bytes 32768 | tf_op jit(solution)/shard_map/all_to_all | solution.py:338
  13.9 0.0 collective-permute-done.2.refs_3_
  13.9 0.0 collective-permute-done.1.refs_2_
  14.0 0.0 collective-permute-done.refs_1_
  14.0 0.5 %collective-permute-start.3 = (f32[32,768]{1,0:T(8,128)S(1)}, f32[32,768]{1,0:T(8,128)}, u32[]{:S(2)}, u32[]{:S(2)}) collective-permute-start(f32[32,768]{1,0:T(8,128)S(1)} %join.1.refs_3_.refs_4_.refs_5_.refs_6_), channel_id=1, source_target_pairs={{0,1},{1,0},{2,3},{3,2},{4,5},{5,4},{6,7},{7,6},{8,9},{9,8},{10,11... | collective-permute-start | bytes 294920 | tf_op jit(solution)/shard_map/ppermute | solution.py:370
  14.4 4.2 %all-to-all-done.refs_0_ = s32[32,1,128]{2,1,0:T(1,128)S(1)} async-done(((s32[32,1,128]{2,1,0:T(1,128)}), s32[32,1,128]{2,1,0:T(1,128)S(1)}, u32[]{:S(2)}, u32[]{:S(2)}) %all-to-all-start) | async-done | bytes 16416 | tf_op jit(solution)/shard_map/all_to_all | solution.py:338
  18.7 0.0 copy-done.3
  18.7 1.2 %rows.1 = bf16[32,8,384]{2,1,0:T(8,128)(2,1)} custom-call(s32[32,1,128]{2,1,0:T(1,128)S(1)} %all-to-all-done.refs_0_, f32[1024,768]{1,0:T(8,128)S(1)} %copy-done.3), custom_call_target="tpu_custom_call" | custom-call | flops 1000000000 | bytes 4194304 | tf_op jit(solution)/shard_map/rows/pallas_call | solution.py:349
  19.9 4.9 %all-to-all-start.1 = ((bf16[32,8,384]{2,1,0:T(8,128)(2,1)}), bf16[32,8,384]{2,1,0:T(8,128)(2,1)S(1)}, u32[]{:S(2)}, u32[]{:S(2)}) async-start(bf16[32,8,384]{2,1,0:T(8,128)(2,1)} %rows.1), calls=%async_computation.1 | async-start | bytes 393216 | tf_op jit(solution)/shard_map/all_to_all | solution.py:358
  24.8 0.0 collective-permute-done.3.refs_7_.refs_8_.refs_9_.refs_10_
  24.8 0.0 copy-start.4
  24.8 1.1 %copy-done.4 = f32[96,256,8]{1,2,0:T(8,128)S(1)} copy-done((f32[96,256,8]{1,2,0:T(8,128)S(1)}, f32[96,256,8]{1,2,0:T(8,128)}, u32[]{:S(2)}) %copy-start.4) | copy-done | bytes 786456
  25.9 0.0 copy-start.5
  25.9 1.1 %copy-done.5 = s32[8,96,256]{2,1,0:T(8,128)S(1)} copy-done((s32[8,96,256]{2,1,0:T(8,128)S(1)}, s32[8,96,256]{2,1,0:T(8,128)}, u32[]{:S(2)}) %copy-start.5) | copy-done | bytes 786456
  27.1 0.0 copy-start.1
  27.1 0.0 copy-start.2
  27.1 9.9 %pq.1 = f32[8,64,256]{2,1,0:T(8,128)} custom-call(s32[8,128]{1,0:T(8,128)S(1)} %groups.1.refs_0_, f32[768,256]{1,0:T(8,128)S(1)} %bitcast.5, s32[8,96,256]{2,1,0:T(8,128)S(1)} %copy-done.5, f32[32,768]{1,0:T(8,128)S(1)} %join.1.refs_3_.refs_4_.refs_5_.refs_6_, f32[32,768]{1,0:T(8,128)S(1)} %join.1.refs_3_.refs_4_.refs_5_.refs_6_, ...), custom_call_target="tpu_custom_call" | custom-call | flops 10000000000 | bytes 31457280 | tf_op jit(solution)/shard_map/pq/pallas_call | solution.py:379
  37.0 0.0 all-to-all-done.1.refs_3_
  37.0 0.0 copy-done.1
  37.0 0.0 copy-done.2
  37.0 1.0 %final.1 = f32[8,16]{1,0:T(8,128)} custom-call(s32[8,16]{1,0:T(8,128)S(1)} %copy-done.1, s32[8,16]{1,0:T(8,128)S(1)} %copy-done.2, f32[8,768]{1,0:T(8,128)S(1)} %copy-done, bf16[32,8,384]{2,1,0:T(8,128)(2,1)S(1)} %all-to-all-done.1.refs_3_), custom_call_target="tpu_custom_call" | custom-call | tf_op jit(solution)/shard_map/final/pallas_call | solution.py:405
  (1 shorter events, 0.0 us)
Async XLA Ops:
  0.6 1.0 %copy-start = (f32[8,768]{1,0:T(8,128)S(1)}, f32[8,768]{1,0:T(8,128)}, u32[]{:S(2)}) copy-start(f32[8,768]{1,0:T(8,128)} %refs_2_.3) | copy-start | bytes 73732
  0.6 0.7 %copy-start.6 = (s32[64,8]{0,1:T(8,128)S(1)}, s32[64,8]{0,1:T(8,128)}, u32[]{:S(2)}) copy-start(s32[64,8]{0,1:T(8,128)} %param.10) | copy-start | bytes 6148
  1.7 17.0 %copy-start.3 = (f32[1024,768]{1,0:T(8,128)S(1)}, f32[1024,768]{1,0:T(8,128)}, u32[]{:S(2)}) copy-start(f32[1024,768]{1,0:T(8,128)} %refs_1_.4) | copy-start | bytes 9437188
  1.7 12.3 %collective-permute-start.2 = (f32[8,768]{1,0:T(8,128)S(1)}, f32[8,768]{1,0:T(8,128)S(1)}, u32[]{:S(2)}, u32[]{:S(2)}) collective-permute-start(f32[8,768]{1,0:T(8,128)S(1)} %copy-done), channel_id=1, source_target_pairs={{0,6},{1,7},{2,4},{3,5},{4,2},{5,3},{6,0},{7,1},{8,14},{9,15},{10,... | collective-permute-start | bytes 73736 | tf_op jit(solution)/shard_map/ppermute | solution.py:343
  3.0 10.9 %collective-permute-start.1 = (f32[8,768]{1,0:T(8,128)S(1)}, f32[8,768]{1,0:T(8,128)S(1)}, u32[]{:S(2)}, u32[]{:S(2)}) collective-permute-start(f32[8,768]{1,0:T(8,128)S(1)} %copy-done), channel_id=1, source_target_pairs={{0,4},{1,5},{2,6},{3,7},{4,0},{5,1},{6,2},{7,3},{8,12},{9,13},{10,... | collective-permute-start | bytes 73736 | tf_op jit(solution)/shard_map/ppermute | solution.py:343
  4.1 9.8 %collective-permute-start = (f32[8,768]{1,0:T(8,128)S(1)}, f32[8,768]{1,0:T(8,128)S(1)}, u32[]{:S(2)}, u32[]{:S(2)}) collective-permute-start(f32[8,768]{1,0:T(8,128)S(1)} %copy-done), channel_id=1, source_target_pairs={{0,2},{1,3},{2,0},{3,1},{4,6},{5,7},{6,4},{7,5},{8,10},{9,11},{10,... | collective-permute-start | bytes 73736 | tf_op jit(solution)/shard_map/ppermute | solution.py:343
  6.8 11.9 %all-to-all-start = ((s32[32,1,128]{2,1,0:T(1,128)}), s32[32,1,128]{2,1,0:T(1,128)S(1)}, u32[]{:S(2)}, u32[]{:S(2)}) async-start(s32[32,1,128]{2,1,0:T(1,128)} %ids.1), calls=%async_computation | async-start | bytes 32768 | tf_op jit(solution)/shard_map/all_to_all | solution.py:338
  14.0 10.8 %collective-permute-start.3 = (f32[32,768]{1,0:T(8,128)S(1)}, f32[32,768]{1,0:T(8,128)}, u32[]{:S(2)}, u32[]{:S(2)}) collective-permute-start(f32[32,768]{1,0:T(8,128)S(1)} %join.1.refs_3_.refs_4_.refs_5_.refs_6_), channel_id=1, source_target_pairs={{0,1},{1,0},{2,3},{3,2},{4,5},{5,4},{6,7},{7,6},{8,9},{9,8},{10,11... | collective-permute-start | bytes 294920 | tf_op jit(solution)/shard_map/ppermute | solution.py:370
  19.9 17.1 %all-to-all-start.1 = ((bf16[32,8,384]{2,1,0:T(8,128)(2,1)}), bf16[32,8,384]{2,1,0:T(8,128)(2,1)S(1)}, u32[]{:S(2)}, u32[]{:S(2)}) async-start(bf16[32,8,384]{2,1,0:T(8,128)(2,1)} %rows.1), calls=%async_computation.1 | async-start | bytes 393216 | tf_op jit(solution)/shard_map/all_to_all | solution.py:358
  24.8 1.1 %copy-start.4 = (f32[96,256,8]{1,2,0:T(8,128)S(1)}, f32[96,256,8]{1,2,0:T(8,128)}, u32[]{:S(2)}) copy-start(f32[96,256,8]{1,2,0:T(8,128)} %param.8) | copy-start | bytes 2359300
  25.9 1.1 %copy-start.5 = (s32[8,96,256]{2,1,0:T(8,128)S(1)}, s32[8,96,256]{2,1,0:T(8,128)}, u32[]{:S(2)}) copy-start(s32[8,96,256]{2,1,0:T(8,128)} %refs_2_.2) | copy-start | bytes 2359300
  27.1 9.9 %copy-start.1 = (s32[8,16]{1,0:T(8,128)S(1)}, s32[8,16]{1,0:T(8,128)}, u32[]{:S(2)}) copy-start(s32[8,16]{1,0:T(8,128)} %refs_0_.5) | copy-start | bytes 1540
  27.1 9.9 %copy-start.2 = (s32[8,16]{1,0:T(8,128)S(1)}, s32[8,16]{1,0:T(8,128)}, u32[]{:S(2)}) copy-start(s32[8,16]{1,0:T(8,128)} %refs_1_.5) | copy-start | bytes 1540

commit v2 on v1

--- a/solution.py
+++ b/solution.py
@@ -88,7 +88,7 @@
         out_ref[block * LANE : block * LANE + count] = turned.reshape(count, 1, LANE)
 
 
-def paired_rows_kernel(ids_ref, vectors_ref, out_ref):
+def paired_rows_kernel(ids_ref, vectors_ref, out_ref, buffer, sems):
     sources, slots, piece = out_ref.shape
     count = vectors_ref.shape[0]
     pairs = sources // 2
@@ -104,22 +104,30 @@
         lane = lax.broadcasted_iota(jnp.int32, (pairs * SUB, LANE), 1) + block * LANE
         chosen.append(jnp.where(wanted == lane, 1.0, 0.0).astype(jnp.bfloat16))
     chosen = jnp.concatenate(chosen, axis=1)
-    found = []
-    for part in range(2):
-        vectors = vectors_ref[:, part * piece : (part + 1) * piece].astype(jnp.bfloat16)
-        product = jnp.dot(chosen, vectors, preferred_element_type=jnp.float32)
-        found.append(product.reshape(pairs, SUB, piece))
-    swapped = [pltpu.roll(x, SUB // 2, axis=1) for x in found]
-    upper = lax.broadcasted_iota(jnp.int32, (pairs, SUB, piece), 1) < SUB // 2
-    even = jnp.where(upper, found[0], swapped[1])
-    odd = jnp.where(upper, swapped[0], found[1])
-    result = jnp.stack([even, odd], axis=1).reshape(sources, slots, piece)
-    out_ref[...] = result.astype(jnp.bfloat16)
+    upper = lax.broadcasted_iota(jnp.int32, (pairs, SUB, LANE), 1) < SUB // 2
+    copies = []
+    for step in range(piece // LANE):
+        found = []
+        for part in range(2):
+            start = part * piece + step * LANE
+            found.append(vectors_ref[:, start : start + LANE].astype(jnp.bfloat16))
+        product = jnp.dot(
+            chosen, jnp.concatenate(found, axis=1), preferred_element_type=jnp.float32
+        )
+        found = [product[:, p * LANE : (p + 1) * LANE].reshape(pairs, SUB, LANE) for p in (0, 1)]
+        swapped = [pltpu.roll(x, SUB // 2, axis=1) for x in found]
+        even = jnp.where(upper, found[0], swapped[1])
+        odd = jnp.where(upper, swapped[0], found[1])
+        result = jnp.stack([even, odd], axis=1).reshape(sources, slots, LANE)
+        buffer[step] = result.astype(jnp.bfloat16)
+        target = out_ref.at[:, :, step * LANE : (step + 1) * LANE]
+        copies.append(pltpu.make_async_copy(buffer.at[step], target, sems.at[step]))
+        copies[-1].start()
+    for copy in copies:
+        copy.wait()
 
 
 def rows_kernel(capacity, parts, ids_ref, vectors_ref, out_ref):
-    if capacity * 2 == SUB and parts == 2 and out_ref.shape[0] % 2 == 0:
-        return paired_rows_kernel(ids_ref, vectors_ref, out_ref)
     sources, slots = out_ref.shape[0], out_ref.shape[1]
     count, width = vectors_ref.shape
     piece = width // parts
@@ -204,7 +212,7 @@
 
 def pq_kernel(q_dev, pieces, unroll, lists_hbm, codebook_ref, wide_codes, *refs):
     number = len(pieces)
-    chunk_refs, (out_ref, queries, table, codes, lists_s, sems) = (
+    chunk_refs, (out_ref, queries, spread, table, codes, lists_s, sems) = (
         refs[:number],
         refs[number:],
     )
@@ -226,8 +234,8 @@
 
     half = LANE // 2
     lane = lax.broadcasted_iota(jnp.int32, (total, LANE), 1)
-    inside = lax.broadcasted_iota(jnp.int32, (1, SUB, LANE), 2) % half // (half // SUB)
-    own = jnp.where(inside == lax.broadcasted_iota(jnp.int32, (1, SUB, LANE), 1), 1.0, 0.0)
+    inside = lax.broadcasted_iota(jnp.int32, (SUB, LANE), 1) % half // (half // SUB)
+    own = jnp.where(inside == lax.broadcasted_iota(jnp.int32, (SUB, LANE), 0), 1.0, 0.0)
 
     def columns(k, carry):
         x = queries[:, pl.ds(pl.multiple_of(k * LANE, LANE), LANE)]
@@ -236,10 +244,14 @@
         for side in range(2):
             wide = jnp.where((lane < half) == (side == 0), x, swapped)
             high = wide.astype(jnp.bfloat16).astype(jnp.float32)
+            spread[0] = high
+            spread[1] = wide - high
             terms = []
-            for term in (high, wide - high):
-                spread = (term[:, None, :] * own).reshape(total * SUB, LANE)
-                terms.append(spread.astype(jnp.bfloat16))
+            for term in range(2):
+                lines = [
+                    spread[term, pl.ds(q, SUB, stride=0), :] * own for q in range(total)
+                ]
+                terms.append(jnp.concatenate(lines, axis=0).astype(jnp.bfloat16))
             c = codebook_ref[pl.ds(pl.multiple_of(k * LANE + side * half, half), half), :]
             c_high = c.astype(jnp.bfloat16)
             c_low = (c - c_high.astype(jnp.float32)).astype(jnp.bfloat16)
@@ -346,11 +358,21 @@
     else:
         gathered = lax.all_gather(queries, "shard", axis=0, tiled=True)
 
+    paired = capacity * 2 == SUB and parts == 2 and owners % 2 == 0
+    piece = width // parts
+    kernel, scratch = lambda *refs: rows_kernel(capacity, parts, *refs), []
+    if paired:
+        kernel = paired_rows_kernel
+        scratch = [
+            pltpu.VMEM((piece // LANE, owners, SUB, LANE), jnp.bfloat16),
+            pltpu.SemaphoreType.DMA((piece // LANE,)),
+        ]
     rows = pl.pallas_call(
-        lambda *refs: rows_kernel(capacity, parts, *refs),
-        out_shape=jax.ShapeDtypeStruct((owners, SUB, width // parts), jnp.bfloat16),
+        kernel,
+        out_shape=jax.ShapeDtypeStruct((owners, SUB, piece), jnp.bfloat16),
         in_specs=[whole()] * 2,
-        out_specs=whole(),
+        out_specs=whole(pl.ANY) if paired else whole(),
+        scratch_shapes=scratch,
         name="rows",
         compiler_params=pltpu.CompilerParams(vmem_limit_bytes=16 << 20),
         cost_estimate=pl.CostEstimate(flops=10**9, bytes_accessed=4 << 20, transcendentals=0),
@@ -383,6 +405,7 @@
         out_specs=whole(),
         scratch_shapes=[
             pltpu.VMEM((total, width), jnp.float32),
+            pltpu.VMEM((2, total, LANE), jnp.float32),
             pltpu.VMEM((total, subs // SUB // 2, 2 * SUB, centres), jnp.bfloat16),
             pltpu.VMEM((lists, subs, entries), jnp.int16),
             pltpu.SMEM((lists, list_width), jnp.int32),

time: 38.4 us -> 38.3 us (level)
  no operation moved by 1% of the time
where the time goes in v2:
time: 38.3 us; the launch traced here: 37.8 us
  starting transfers between devices  16.1 us (42%)
  Pallas kernels  13.8 us (36%)
  waiting for transfers between devices  4.25 us (11%)
  local copies, waits for them, and re-layouts  2.96 us (8%)
  between operations  0.78 us (2%)
    pallas_call x1, Pallas kernels, per_device(): pl.pallas_call(lambda *refs: pq_kernel(q_dev, pieces, unroll, *refs), out...  9.83 us
    all_to_all x1, starting transfers between devices, per_device(): asked = lax.all_to_all(ids, AXES, split_axis=0, concat_axis=0, tiled=True)  7.16 us
    all_to_all x1, starting transfers between devices, per_device(): lax.all_to_all(rows, AXES, split_axis=0, concat_axis=0, tiled=True)  4.9 us
    all_to_all x1, waiting for transfers between devices, per_device(): asked = lax.all_to_all(ids, AXES, split_axis=0, concat_axis=0, tiled=True)  4.24 us
    ppermute x3, starting transfers between devices, per_device(): lax.ppermute(own, 'shard', [(i, i ^ k) for i in range(shards)])  3.56 us
    unnamed x14, local copies, waits for them, and re-layouts  2.96 us
    pallas_call x1, Pallas kernels, per_device(): pl.pallas_call(lambda *refs: ids_kernel(capacity, parts, *refs), out_shap...  1.53 us
    pallas_call x1, Pallas kernels, per_device(): pl.pallas_call(kernel, out_shape=jax.ShapeDtypeStruct((owners, SUB, piece...  1.12 us
  transfers between devices with their start and end apart: 6, of which 1 were waited for; matrix products, arithmetic and copies ran while one was open for 0% of the time, Pallas kernels for 33%

profile of v2, /device:TPU:13, one launch (start us, length us, event | category | flops | bytes accessed | tf_op | source)
XLA Modules:
  0.0 37.8 jit_solution(10356457757630144312)
XLA Ops:
  0.6 0.0 copy-start
  0.6 0.0 copy-start.6
  0.6 0.7 %copy-done.6 = s32[64,8]{0,1:T(8,128)S(1)} copy-done((s32[64,8]{0,1:T(8,128)S(1)}, s32[64,8]{0,1:T(8,128)}, u32[]{:S(2)}) %copy-start.6) | copy-done | bytes 2072
  1.3 0.3 groups.1.refs_0_
  1.6 0.0 copy-done
  1.7 0.0 copy-start.3
  1.7 1.4 %collective-permute-start.2 = (f32[8,768]{1,0:T(8,128)S(1)}, f32[8,768]{1,0:T(8,128)S(1)}, u32[]{:S(2)}, u32[]{:S(2)}) collective-permute-start(f32[8,768]{1,0:T(8,128)S(1)} %copy-done), channel_id=1, source_target_pairs={{0,6},{1,7},{2,4},{3,5},{4,2},{5,3},{6,0},{7,1},{8,14},{9,15},{10,... | collective-permute-start | bytes 73736 | tf_op jit(solution)/shard_map/ppermute | solution.py:355
  3.0 1.1 %collective-permute-start.1 = (f32[8,768]{1,0:T(8,128)S(1)}, f32[8,768]{1,0:T(8,128)S(1)}, u32[]{:S(2)}, u32[]{:S(2)}) collective-permute-start(f32[8,768]{1,0:T(8,128)S(1)} %copy-done), channel_id=1, source_target_pairs={{0,4},{1,5},{2,6},{3,7},{4,0},{5,1},{6,2},{7,3},{8,12},{9,13},{10,... | collective-permute-start | bytes 73736 | tf_op jit(solution)/shard_map/ppermute | solution.py:355
  4.1 1.1 %collective-permute-start = (f32[8,768]{1,0:T(8,128)S(1)}, f32[8,768]{1,0:T(8,128)S(1)}, u32[]{:S(2)}, u32[]{:S(2)}) collective-permute-start(f32[8,768]{1,0:T(8,128)S(1)} %copy-done), channel_id=1, source_target_pairs={{0,2},{1,3},{2,0},{3,1},{4,6},{5,7},{6,4},{7,5},{8,10},{9,11},{10,... | collective-permute-start | bytes 73736 | tf_op jit(solution)/shard_map/ppermute | solution.py:355
  5.2 1.5 %ids.1 = s32[32,1,128]{2,1,0:T(1,128)} custom-call(s32[8,16]{1,0:T(8,128)} %refs_0_.5, s32[8,16]{1,0:T(8,128)} %refs_1_.3), custom_call_target="tpu_custom_call" | custom-call | flops 1000000000 | bytes 6291456 | tf_op jit(solution)/shard_map/ids/pallas_call | solution.py:330
  6.8 7.2 %all-to-all-start = ((s32[32,1,128]{2,1,0:T(1,128)}), s32[32,1,128]{2,1,0:T(1,128)S(1)}, u32[]{:S(2)}, u32[]{:S(2)}) async-start(s32[32,1,128]{2,1,0:T(1,128)} %ids.1), calls=%async_computation | async-start | bytes 32768 | tf_op jit(solution)/shard_map/all_to_all | solution.py:350
  13.9 0.0 collective-permute-done.2.refs_3_
  13.9 0.0 collective-permute-done.1.refs_2_
  14.0 0.0 collective-permute-done.refs_1_
  14.0 0.5 %collective-permute-start.3 = (f32[32,768]{1,0:T(8,128)S(1)}, f32[32,768]{1,0:T(8,128)}, u32[]{:S(2)}, u32[]{:S(2)}) collective-permute-start(f32[32,768]{1,0:T(8,128)S(1)} %join.1.refs_3_.refs_4_.refs_5_.refs_6_), channel_id=1, source_target_pairs={{0,1},{1,0},{2,3},{3,2},{4,5},{5,4},{6,7},{7,6},{8,9},{9,8},{10,11... | collective-permute-start | bytes 294920 | tf_op jit(solution)/shard_map/ppermute | solution.py:392
  14.4 4.2 %all-to-all-done.ids_ref = s32[32,1,128]{2,1,0:T(1,128)S(1)} async-done(((s32[32,1,128]{2,1,0:T(1,128)}), s32[32,1,128]{2,1,0:T(1,128)S(1)}, u32[]{:S(2)}, u32[]{:S(2)}) %all-to-all-start) | async-done | bytes 16416 | tf_op jit(solution)/shard_map/all_to_all | solution.py:350
  18.7 0.0 copy-done.3
  18.7 1.1 %rows.1 = bf16[32,8,384]{2,1,0:T(8,128)(2,1)} custom-call(s32[32,1,128]{2,1,0:T(1,128)S(1)} %all-to-all-done.ids_ref, f32[1024,768]{1,0:T(8,128)S(1)} %copy-done.3), custom_call_target="tpu_custom_call" | custom-call | flops 1000000000 | bytes 4194304 | tf_op jit(solution)/shard_map/rows/pallas_call | solution.py:370
  19.8 4.9 %all-to-all-start.1 = ((bf16[32,8,384]{2,1,0:T(8,128)(2,1)}), bf16[32,8,384]{2,1,0:T(8,128)(2,1)S(1)}, u32[]{:S(2)}, u32[]{:S(2)}) async-start(bf16[32,8,384]{2,1,0:T(8,128)(2,1)} %rows.1), calls=%async_computation.1 | async-start | bytes 393216 | tf_op jit(solution)/shard_map/all_to_all | solution.py:380
  24.7 0.0 collective-permute-done.3.refs_7_.refs_8_.refs_9_.refs_10_
  24.7 0.0 copy-start.4
  24.7 1.1 %copy-done.4 = f32[96,256,8]{1,2,0:T(8,128)S(1)} copy-done((f32[96,256,8]{1,2,0:T(8,128)S(1)}, f32[96,256,8]{1,2,0:T(8,128)}, u32[]{:S(2)}) %copy-start.4) | copy-done | bytes 786456
  25.9 0.0 copy-start.5
  25.9 1.1 %copy-done.5 = s32[8,96,256]{2,1,0:T(8,128)S(1)} copy-done((s32[8,96,256]{2,1,0:T(8,128)S(1)}, s32[8,96,256]{2,1,0:T(8,128)}, u32[]{:S(2)}) %copy-start.5) | copy-done | bytes 786456
  27.0 0.0 copy-start.1
  27.0 0.0 copy-start.2
  27.0 9.8 %pq.1 = f32[8,64,256]{2,1,0:T(8,128)} custom-call(s32[8,128]{1,0:T(8,128)S(1)} %groups.1.refs_0_, f32[768,256]{1,0:T(8,128)S(1)} %bitcast.5, s32[8,96,256]{2,1,0:T(8,128)S(1)} %copy-done.5, f32[32,768]{1,0:T(8,128)S(1)} %join.1.refs_3_.refs_4_.refs_5_.refs_6_, f32[32,768]{1,0:T(8,128)S(1)} %join.1.refs_3_.refs_4_.refs_5_.refs_6_, ...), custom_call_target="tpu_custom_call" | custom-call | flops 10000000000 | bytes 31457280 | tf_op jit(solution)/shard_map/pq/pallas_call | solution.py:401
  36.8 0.0 all-to-all-done.1.refs_3_
  36.9 0.0 copy-done.1
  36.9 0.0 copy-done.2
  36.9 1.0 %final.1 = f32[8,16]{1,0:T(8,128)} custom-call(s32[8,16]{1,0:T(8,128)S(1)} %copy-done.1, s32[8,16]{1,0:T(8,128)S(1)} %copy-done.2, f32[8,768]{1,0:T(8,128)S(1)} %copy-done, bf16[32,8,384]{2,1,0:T(8,128)(2,1)S(1)} %all-to-all-done.1.refs_3_), custom_call_target="tpu_custom_call" | custom-call | tf_op jit(solution)/shard_map/final/pallas_call | solution.py:428
  (1 shorter events, 0.0 us)
Async XLA Ops:
  0.6 1.0 %copy-start = (f32[8,768]{1,0:T(8,128)S(1)}, f32[8,768]{1,0:T(8,128)}, u32[]{:S(2)}) copy-start(f32[8,768]{1,0:T(8,128)} %refs_2_.3) | copy-start | bytes 73732
  0.6 0.7 %copy-start.6 = (s32[64,8]{0,1:T(8,128)S(1)}, s32[64,8]{0,1:T(8,128)}, u32[]{:S(2)}) copy-start(s32[64,8]{0,1:T(8,128)} %param.10) | copy-start | bytes 6148
  1.7 17.0 %copy-start.3 = (f32[1024,768]{1,0:T(8,128)S(1)}, f32[1024,768]{1,0:T(8,128)}, u32[]{:S(2)}) copy-start(f32[1024,768]{1,0:T(8,128)} %vectors_ref.1) | copy-start | bytes 9437188
  1.7 12.3 %collective-permute-start.2 = (f32[8,768]{1,0:T(8,128)S(1)}, f32[8,768]{1,0:T(8,128)S(1)}, u32[]{:S(2)}, u32[]{:S(2)}) collective-permute-start(f32[8,768]{1,0:T(8,128)S(1)} %copy-done), channel_id=1, source_target_pairs={{0,6},{1,7},{2,4},{3,5},{4,2},{5,3},{6,0},{7,1},{8,14},{9,15},{10,... | collective-permute-start | bytes 73736 | tf_op jit(solution)/shard_map/ppermute | solution.py:355
  3.0 10.9 %collective-permute-start.1 = (f32[8,768]{1,0:T(8,128)S(1)}, f32[8,768]{1,0:T(8,128)S(1)}, u32[]{:S(2)}, u32[]{:S(2)}) collective-permute-start(f32[8,768]{1,0:T(8,128)S(1)} %copy-done), channel_id=1, source_target_pairs={{0,4},{1,5},{2,6},{3,7},{4,0},{5,1},{6,2},{7,3},{8,12},{9,13},{10,... | collective-permute-start | bytes 73736 | tf_op jit(solution)/shard_map/ppermute | solution.py:355
  4.1 9.8 %collective-permute-start = (f32[8,768]{1,0:T(8,128)S(1)}, f32[8,768]{1,0:T(8,128)S(1)}, u32[]{:S(2)}, u32[]{:S(2)}) collective-permute-start(f32[8,768]{1,0:T(8,128)S(1)} %copy-done), channel_id=1, source_target_pairs={{0,2},{1,3},{2,0},{3,1},{4,6},{5,7},{6,4},{7,5},{8,10},{9,11},{10,... | collective-permute-start | bytes 73736 | tf_op jit(solution)/shard_map/ppermute | solution.py:355
  6.8 11.9 %all-to-all-start = ((s32[32,1,128]{2,1,0:T(1,128)}), s32[32,1,128]{2,1,0:T(1,128)S(1)}, u32[]{:S(2)}, u32[]{:S(2)}) async-start(s32[32,1,128]{2,1,0:T(1,128)} %ids.1), calls=%async_computation | async-start | bytes 32768 | tf_op jit(solution)/shard_map/all_to_all | solution.py:350
  14.0 10.7 %collective-permute-start.3 = (f32[32,768]{1,0:T(8,128)S(1)}, f32[32,768]{1,0:T(8,128)}, u32[]{:S(2)}, u32[]{:S(2)}) collective-permute-start(f32[32,768]{1,0:T(8,128)S(1)} %join.1.refs_3_.refs_4_.refs_5_.refs_6_), channel_id=1, source_target_pairs={{0,1},{1,0},{2,3},{3,2},{4,5},{5,4},{6,7},{7,6},{8,9},{9,8},{10,11... | collective-permute-start | bytes 294920 | tf_op jit(solution)/shard_map/ppermute | solution.py:392
  19.8 17.0 %all-to-all-start.1 = ((bf16[32,8,384]{2,1,0:T(8,128)(2,1)}), bf16[32,8,384]{2,1,0:T(8,128)(2,1)S(1)}, u32[]{:S(2)}, u32[]{:S(2)}) async-start(bf16[32,8,384]{2,1,0:T(8,128)(2,1)} %rows.1), calls=%async_computation.1 | async-start | bytes 393216 | tf_op jit(solution)/shard_map/all_to_all | solution.py:380
  24.7 1.1 %copy-start.4 = (f32[96,256,8]{1,2,0:T(8,128)S(1)}, f32[96,256,8]{1,2,0:T(8,128)}, u32[]{:S(2)}) copy-start(f32[96,256,8]{1,2,0:T(8,128)} %param.8) | copy-start | bytes 2359300
  25.9 1.1 %copy-start.5 = (s32[8,96,256]{2,1,0:T(8,128)S(1)}, s32[8,96,256]{2,1,0:T(8,128)}, u32[]{:S(2)}) copy-start(s32[8,96,256]{2,1,0:T(8,128)} %refs_2_.2) | copy-start | bytes 2359300
  27.0 9.9 %copy-start.1 = (s32[8,16]{1,0:T(8,128)S(1)}, s32[8,16]{1,0:T(8,128)}, u32[]{:S(2)}) copy-start(s32[8,16]{1,0:T(8,128)} %refs_0_.5) | copy-start | bytes 1540
  27.0 9.9 %copy-start.2 = (s32[8,16]{1,0:T(8,128)S(1)}, s32[8,16]{1,0:T(8,128)}, u32[]{:S(2)}) copy-start(s32[8,16]{1,0:T(8,128)} %refs_1_.3) | copy-start | bytes 1540

commit v3 on v2

--- a/solution.py
+++ b/solution.py
@@ -277,32 +277,40 @@
             ]
             out_ref[n, pl.ds(chosen[u], 1), :] = jnp.concatenate(line, axis=1)
 
+    def group(n, begin, size, inner):
+        chosen = [lists_s[n, begin + u] for u in range(size)]
+        sums = [None] * (size * halves)
+        for i in range(blocks):
+            for h in range(halves):
+                code = codes[n, i * rows : (i + 1) * rows, h * LANE : (h + 1) * LANE]
+                low = jnp.bitwise_and(code, jnp.int16(LANE - 1))
+                for u in range(size):
+                    value = pick(table[chosen[u], i, :, 0:LANE], low)
+                    for part in range(1, centres // LANE):
+                        other = pick(table[chosen[u], i, :, part * LANE : (part + 1) * LANE], low)
+                        value = jnp.where(code >= jnp.int16(part * LANE), other, value)
+                    value = value.astype(jnp.float32)
+                    value = value[:SUB] + value[SUB:]
+                    at = u * halves + h
+                    sums[at] = value if i == 0 else sums[at] + value
+            if i == 1:
+                emit(*inner)
+        chosen += chosen[-1:] * (unroll - size)
+        sums += sums[-halves:] * (unroll - size)
+        return n, tuple(chosen), tuple(sums)
+
+    short = unroll // 2
+
     def one_list(n, carry):
         count = lists_s[n, width - 1]
-
-        def some(step, inner):
-            chosen = tuple(lists_s[n, step * unroll + u] for u in range(unroll))
-            sums = [None] * (unroll * halves)
-            for i in range(blocks):
-                for h in range(halves):
-                    code = codes[n, i * rows : (i + 1) * rows, h * LANE : (h + 1) * LANE]
-                    low = jnp.bitwise_and(code, jnp.int16(LANE - 1))
-                    for u in range(unroll):
-                        value = pick(table[chosen[u], i, :, 0:LANE], low)
-                        for part in range(1, centres // LANE):
-                            other = pick(
-                                table[chosen[u], i, :, part * LANE : (part + 1) * LANE], low
-                            )
-                            value = jnp.where(code >= jnp.int16(part * LANE), other, value)
-                        value = value.astype(jnp.float32)
-                        value = value[:SUB] + value[SUB:]
-                        at = u * halves + h
-                        sums[at] = value if i == 0 else sums[at] + value
-                if i == 1:
-                    emit(*inner)
-            return n, chosen, tuple(sums)
-
-        return lax.fori_loop(0, (count + unroll - 1) // unroll, some, carry)
+        steps = (count + unroll - short - 1) // unroll
+        carry = lax.fori_loop(
+            0, steps, lambda step, inner: group(n, step * unroll, unroll, inner), carry
+        )
+        left = (count - steps * unroll > 0).astype(jnp.int32)
+        return lax.fori_loop(
+            0, left, lambda step, inner: group(n, steps * unroll, short, inner), carry
+        )
 
     first = (
         jnp.int32(0),

time: 38.3 us -> 38 us (level)
  transfers between devices with their start and end apart: 6 -> 6, of which waited for: 1 -> 1; matrix products, arithmetic and copies ran while one was open for 0% -> 0% of each run, Pallas kernels for 33% -> 32%
where the time goes in v3:
time: 38 us; the launch traced here: 37.6 us
  starting transfers between devices  16.1 us (42%)
  Pallas kernels  13.5 us (36%)
  waiting for transfers between devices  4.25 us (11%)
  local copies, waits for them, and re-layouts  2.96 us (8%)
  between operations  0.78 us (2%)
    pallas_call x1, Pallas kernels, per_device(): pl.pallas_call(lambda *refs: pq_kernel(q_dev, pieces, unroll, *refs), out...  9.54 us
    all_to_all x1, starting transfers between devices, per_device(): asked = lax.all_to_all(ids, AXES, split_axis=0, concat_axis=0, tiled=True)  7.16 us
    all_to_all x1, starting transfers between devices, per_device(): lax.all_to_all(rows, AXES, split_axis=0, concat_axis=0, tiled=True)  4.9 us
    all_to_all x1, waiting for transfers between devices, per_device(): asked = lax.all_to_all(ids, AXES, split_axis=0, concat_axis=0, tiled=True)  4.24 us
    ppermute x3, starting transfers between devices, per_device(): lax.ppermute(own, 'shard', [(i, i ^ k) for i in range(shards)])  3.56 us
    unnamed x14, local copies, waits for them, and re-layouts  2.96 us
    pallas_call x1, Pallas kernels, per_device(): pl.pallas_call(lambda *refs: ids_kernel(capacity, parts, *refs), out_shap...  1.53 us
    pallas_call x1, Pallas kernels, per_device(): pl.pallas_call(kernel, out_shape=jax.ShapeDtypeStruct((owners, SUB, piece...  1.12 us
  transfers between devices with their start and end apart: 6, of which 1 were waited for; matrix products, arithmetic and copies ran while one was open for 0% of the time, Pallas kernels for 32%

profile of v3, /device:TPU:13, one launch (start us, length us, event | category | flops | bytes accessed | tf_op | source)
XLA Modules:
  0.0 37.6 jit_solution(17293471776162164631)
XLA Ops:
  0.6 0.0 copy-start
  0.6 0.0 copy-start.6
  0.6 0.7 %copy-done.6 = s32[64,8]{0,1:T(8,128)S(1)} copy-done((s32[64,8]{0,1:T(8,128)S(1)}, s32[64,8]{0,1:T(8,128)}, u32[]{:S(2)}) %copy-start.6) | copy-done | bytes 2072
  1.3 0.3 groups.1.refs_0_
  1.6 0.0 copy-done
  1.7 0.0 copy-start.3
  1.7 1.4 %collective-permute-start.2 = (f32[8,768]{1,0:T(8,128)S(1)}, f32[8,768]{1,0:T(8,128)S(1)}, u32[]{:S(2)}, u32[]{:S(2)}) collective-permute-start(f32[8,768]{1,0:T(8,128)S(1)} %copy-done), channel_id=1, source_target_pairs={{0,6},{1,7},{2,4},{3,5},{4,2},{5,3},{6,0},{7,1},{8,14},{9,15},{10,... | collective-permute-start | bytes 73736 | tf_op jit(solution)/shard_map/ppermute | solution.py:363
  3.0 1.1 %collective-permute-start.1 = (f32[8,768]{1,0:T(8,128)S(1)}, f32[8,768]{1,0:T(8,128)S(1)}, u32[]{:S(2)}, u32[]{:S(2)}) collective-permute-start(f32[8,768]{1,0:T(8,128)S(1)} %copy-done), channel_id=1, source_target_pairs={{0,4},{1,5},{2,6},{3,7},{4,0},{5,1},{6,2},{7,3},{8,12},{9,13},{10,... | collective-permute-start | bytes 73736 | tf_op jit(solution)/shard_map/ppermute | solution.py:363
  4.1 1.1 %collective-permute-start = (f32[8,768]{1,0:T(8,128)S(1)}, f32[8,768]{1,0:T(8,128)S(1)}, u32[]{:S(2)}, u32[]{:S(2)}) collective-permute-start(f32[8,768]{1,0:T(8,128)S(1)} %copy-done), channel_id=1, source_target_pairs={{0,2},{1,3},{2,0},{3,1},{4,6},{5,7},{6,4},{7,5},{8,10},{9,11},{10,... | collective-permute-start | bytes 73736 | tf_op jit(solution)/shard_map/ppermute | solution.py:363
  5.2 1.5 %ids.1 = s32[32,1,128]{2,1,0:T(1,128)} custom-call(s32[8,16]{1,0:T(8,128)} %refs_0_.5, s32[8,16]{1,0:T(8,128)} %refs_1_.3), custom_call_target="tpu_custom_call" | custom-call | flops 1000000000 | bytes 6291456 | tf_op jit(solution)/shard_map/ids/pallas_call | solution.py:338
  6.8 7.2 %all-to-all-start = ((s32[32,1,128]{2,1,0:T(1,128)}), s32[32,1,128]{2,1,0:T(1,128)S(1)}, u32[]{:S(2)}, u32[]{:S(2)}) async-start(s32[32,1,128]{2,1,0:T(1,128)} %ids.1), calls=%async_computation | async-start | bytes 32768 | tf_op jit(solution)/shard_map/all_to_all | solution.py:358
  13.9 0.0 collective-permute-done.2.refs_3_
  13.9 0.0 collective-permute-done.1.refs_2_
  14.0 0.0 collective-permute-done.refs_1_
  14.0 0.5 %collective-permute-start.3 = (f32[32,768]{1,0:T(8,128)S(1)}, f32[32,768]{1,0:T(8,128)}, u32[]{:S(2)}, u32[]{:S(2)}) collective-permute-start(f32[32,768]{1,0:T(8,128)S(1)} %join.1.refs_3_.refs_4_.refs_5_.refs_6_), channel_id=1, source_target_pairs={{0,1},{1,0},{2,3},{3,2},{4,5},{5,4},{6,7},{7,6},{8,9},{9,8},{10,11... | collective-permute-start | bytes 294920 | tf_op jit(solution)/shard_map/ppermute | solution.py:400
  14.4 4.2 %all-to-all-done.ids_ref = s32[32,1,128]{2,1,0:T(1,128)S(1)} async-done(((s32[32,1,128]{2,1,0:T(1,128)}), s32[32,1,128]{2,1,0:T(1,128)S(1)}, u32[]{:S(2)}, u32[]{:S(2)}) %all-to-all-start) | async-done | bytes 16416 | tf_op jit(solution)/shard_map/all_to_all | solution.py:358
  18.7 0.0 copy-done.3
  18.7 1.1 %rows.1 = bf16[32,8,384]{2,1,0:T(8,128)(2,1)} custom-call(s32[32,1,128]{2,1,0:T(1,128)S(1)} %all-to-all-done.ids_ref, f32[1024,768]{1,0:T(8,128)S(1)} %copy-done.3), custom_call_target="tpu_custom_call" | custom-call | flops 1000000000 | bytes 4194304 | tf_op jit(solution)/shard_map/rows/pallas_call | solution.py:378
  19.8 4.9 %all-to-all-start.1 = ((bf16[32,8,384]{2,1,0:T(8,128)(2,1)}), bf16[32,8,384]{2,1,0:T(8,128)(2,1)S(1)}, u32[]{:S(2)}, u32[]{:S(2)}) async-start(bf16[32,8,384]{2,1,0:T(8,128)(2,1)} %rows.1), calls=%async_computation.1 | async-start | bytes 393216 | tf_op jit(solution)/shard_map/all_to_all | solution.py:388
  24.7 0.0 collective-permute-done.3.refs_7_.refs_8_.refs_9_.refs_10_
  24.7 0.0 copy-start.4
  24.7 1.1 %copy-done.4 = f32[96,256,8]{1,2,0:T(8,128)S(1)} copy-done((f32[96,256,8]{1,2,0:T(8,128)S(1)}, f32[96,256,8]{1,2,0:T(8,128)}, u32[]{:S(2)}) %copy-start.4) | copy-done | bytes 786456
  25.9 0.0 copy-start.5
  25.9 1.1 %copy-done.5 = s32[8,96,256]{2,1,0:T(8,128)S(1)} copy-done((s32[8,96,256]{2,1,0:T(8,128)S(1)}, s32[8,96,256]{2,1,0:T(8,128)}, u32[]{:S(2)}) %copy-start.5) | copy-done | bytes 786456
  27.0 0.0 copy-start.1
  27.0 0.0 copy-start.2
  27.0 9.5 %pq.1 = f32[8,64,256]{2,1,0:T(8,128)} custom-call(s32[8,128]{1,0:T(8,128)S(1)} %groups.1.refs_0_, f32[768,256]{1,0:T(8,128)S(1)} %bitcast.5, s32[8,96,256]{2,1,0:T(8,128)S(1)} %copy-done.5, f32[32,768]{1,0:T(8,128)S(1)} %join.1.refs_3_.refs_4_.refs_5_.refs_6_, f32[32,768]{1,0:T(8,128)S(1)} %join.1.refs_3_.refs_4_.refs_5_.refs_6_, ...), custom_call_target="tpu_custom_call" | custom-call | flops 10000000000 | bytes 31457280 | tf_op jit(solution)/shard_map/pq/pallas_call | solution.py:409
  36.6 0.0 all-to-all-done.1.refs_3_
  36.6 0.0 copy-done.1
  36.6 0.0 copy-done.2
  36.6 1.0 %final.1 = f32[8,16]{1,0:T(8,128)} custom-call(s32[8,16]{1,0:T(8,128)S(1)} %copy-done.1, s32[8,16]{1,0:T(8,128)S(1)} %copy-done.2, f32[8,768]{1,0:T(8,128)S(1)} %copy-done, bf16[32,8,384]{2,1,0:T(8,128)(2,1)S(1)} %all-to-all-done.1.refs_3_), custom_call_target="tpu_custom_call" | custom-call | tf_op jit(solution)/shard_map/final/pallas_call | solution.py:436
  (1 shorter events, 0.0 us)
Async XLA Ops:
  0.6 1.0 %copy-start = (f32[8,768]{1,0:T(8,128)S(1)}, f32[8,768]{1,0:T(8,128)}, u32[]{:S(2)}) copy-start(f32[8,768]{1,0:T(8,128)} %refs_2_.3) | copy-start | bytes 73732
  0.6 0.7 %copy-start.6 = (s32[64,8]{0,1:T(8,128)S(1)}, s32[64,8]{0,1:T(8,128)}, u32[]{:S(2)}) copy-start(s32[64,8]{0,1:T(8,128)} %param.10) | copy-start | bytes 6148
  1.7 17.0 %copy-start.3 = (f32[1024,768]{1,0:T(8,128)S(1)}, f32[1024,768]{1,0:T(8,128)}, u32[]{:S(2)}) copy-start(f32[1024,768]{1,0:T(8,128)} %vectors_ref.1) | copy-start | bytes 9437188
  1.7 12.3 %collective-permute-start.2 = (f32[8,768]{1,0:T(8,128)S(1)}, f32[8,768]{1,0:T(8,128)S(1)}, u32[]{:S(2)}, u32[]{:S(2)}) collective-permute-start(f32[8,768]{1,0:T(8,128)S(1)} %copy-done), channel_id=1, source_target_pairs={{0,6},{1,7},{2,4},{3,5},{4,2},{5,3},{6,0},{7,1},{8,14},{9,15},{10,... | collective-permute-start | bytes 73736 | tf_op jit(solution)/shard_map/ppermute | solution.py:363
  3.0 10.9 %collective-permute-start.1 = (f32[8,768]{1,0:T(8,128)S(1)}, f32[8,768]{1,0:T(8,128)S(1)}, u32[]{:S(2)}, u32[]{:S(2)}) collective-permute-start(f32[8,768]{1,0:T(8,128)S(1)} %copy-done), channel_id=1, source_target_pairs={{0,4},{1,5},{2,6},{3,7},{4,0},{5,1},{6,2},{7,3},{8,12},{9,13},{10,... | collective-permute-start | bytes 73736 | tf_op jit(solution)/shard_map/ppermute | solution.py:363
  4.1 9.8 %collective-permute-start = (f32[8,768]{1,0:T(8,128)S(1)}, f32[8,768]{1,0:T(8,128)S(1)}, u32[]{:S(2)}, u32[]{:S(2)}) collective-permute-start(f32[8,768]{1,0:T(8,128)S(1)} %copy-done), channel_id=1, source_target_pairs={{0,2},{1,3},{2,0},{3,1},{4,6},{5,7},{6,4},{7,5},{8,10},{9,11},{10,... | collective-permute-start | bytes 73736 | tf_op jit(solution)/shard_map/ppermute | solution.py:363
  6.8 11.9 %all-to-all-start = ((s32[32,1,128]{2,1,0:T(1,128)}), s32[32,1,128]{2,1,0:T(1,128)S(1)}, u32[]{:S(2)}, u32[]{:S(2)}) async-start(s32[32,1,128]{2,1,0:T(1,128)} %ids.1), calls=%async_computation | async-start | bytes 32768 | tf_op jit(solution)/shard_map/all_to_all | solution.py:358
  14.0 10.7 %collective-permute-start.3 = (f32[32,768]{1,0:T(8,128)S(1)}, f32[32,768]{1,0:T(8,128)}, u32[]{:S(2)}, u32[]{:S(2)}) collective-permute-start(f32[32,768]{1,0:T(8,128)S(1)} %join.1.refs_3_.refs_4_.refs_5_.refs_6_), channel_id=1, source_target_pairs={{0,1},{1,0},{2,3},{3,2},{4,5},{5,4},{6,7},{7,6},{8,9},{9,8},{10,11... | collective-permute-start | bytes 294920 | tf_op jit(solution)/shard_map/ppermute | solution.py:400
  19.8 16.7 %all-to-all-start.1 = ((bf16[32,8,384]{2,1,0:T(8,128)(2,1)}), bf16[32,8,384]{2,1,0:T(8,128)(2,1)S(1)}, u32[]{:S(2)}, u32[]{:S(2)}) async-start(bf16[32,8,384]{2,1,0:T(8,128)(2,1)} %rows.1), calls=%async_computation.1 | async-start | bytes 393216 | tf_op jit(solution)/shard_map/all_to_all | solution.py:388
  24.7 1.1 %copy-start.4 = (f32[96,256,8]{1,2,0:T(8,128)S(1)}, f32[96,256,8]{1,2,0:T(8,128)}, u32[]{:S(2)}) copy-start(f32[96,256,8]{1,2,0:T(8,128)} %param.8) | copy-start | bytes 2359300
  25.9 1.1 %copy-start.5 = (s32[8,96,256]{2,1,0:T(8,128)S(1)}, s32[8,96,256]{2,1,0:T(8,128)}, u32[]{:S(2)}) copy-start(s32[8,96,256]{2,1,0:T(8,128)} %refs_2_.2) | copy-start | bytes 2359300
  27.0 9.6 %copy-start.1 = (s32[8,16]{1,0:T(8,128)S(1)}, s32[8,16]{1,0:T(8,128)}, u32[]{:S(2)}) copy-start(s32[8,16]{1,0:T(8,128)} %refs_0_.5) | copy-start | bytes 1540
  27.0 9.6 %copy-start.2 = (s32[8,16]{1,0:T(8,128)S(1)}, s32[8,16]{1,0:T(8,128)}, u32[]{:S(2)}) copy-start(s32[8,16]{1,0:T(8,128)} %refs_1_.3) | copy-start | bytes 1540

commit v4 on v3

--- a/solution.py
+++ b/solution.py
@@ -149,7 +149,7 @@
     out_ref[...] = result.reshape(sources, slots, piece).astype(jnp.bfloat16)
 
 
-def final_kernel(capacity, parts, owner_ref, row_ref, queries_ref, rows_ref, out_ref):
+def final_kernel(capacity, parts, place_ref, queries_ref, rows_ref, out_ref):
     owners, slots, piece = rows_ref.shape
     q_dev, cands = out_ref.shape
     rows = rows_ref[...].reshape(owners * slots, piece)
@@ -165,10 +165,7 @@
             width = scores.shape[1]
             scores = pltpu.roll(scores, width - part * capacity, axis=1)
         total = scores if part == 0 else total + scores
-    owner = owner_ref[...]
-    padded = jnp.concatenate([owner, jnp.zeros((q_dev, LANE - cands), jnp.int32)], axis=1)
-    rank = before(owner_table(owner, row_ref[...], owners))
-    place = padded * slots + pick_wide(rank, padded)
+    place = place_ref[...]
     out_ref[...] = pick_wide(total, place)[:, :cands]
 
 
@@ -178,7 +175,13 @@
         refs[-1][n * rows : (n + 1) * rows] = ref[...]
 
 
-def lists_kernel(lists, probes_ref, out_ref):
+def lists_kernel(lists, owners, probes_ref, owner_ref, row_ref, out_ref, place_ref):
+    q_dev, cands = owner_ref.shape
+    slots = SUB
+    owner = owner_ref[...]
+    padded = jnp.concatenate([owner, jnp.zeros((q_dev, LANE - cands), jnp.int32)], axis=1)
+    rank = before(owner_table(owner, row_ref[...], owners))
+    place_ref[...] = padded * slots + pick_wide(rank, padded)
     total = probes_ref.shape[1]
     width = out_ref.shape[1]
     shard = lax.axis_index("shard")
@@ -345,15 +348,18 @@
     )(cand_owner, cand_row)
     list_width = -(-(total + unroll + 1) // LANE) * LANE
     grouping = pl.pallas_call(
-        lambda *refs: lists_kernel(lists, *refs),
-        out_shape=jax.ShapeDtypeStruct((lists, list_width), jnp.int32),
-        in_specs=[whole()],
-        out_specs=whole(),
+        lambda *refs: lists_kernel(lists, owners, *refs),
+        out_shape=(
+            jax.ShapeDtypeStruct((lists, list_width), jnp.int32),
+            jax.ShapeDtypeStruct((q_dev, LANE), jnp.int32),
+        ),
+        in_specs=[whole()] * 3,
+        out_specs=(whole(), whole()),
         name="groups",
         compiler_params=pltpu.CompilerParams(vmem_limit_bytes=4 << 20),
         cost_estimate=pl.CostEstimate(flops=10**9, bytes_accessed=12 << 20, transcendentals=0),
     )
-    groups = grouping(probes.T)
+    groups, place = grouping(probes.T, cand_owner, cand_row)
     own, groups = lax.optimization_barrier((queries, groups))
     asked = lax.all_to_all(ids, AXES, split_axis=0, concat_axis=0, tiled=True)
 
@@ -436,11 +442,11 @@
     rerank = pl.pallas_call(
         lambda *refs: final_kernel(capacity, parts, *refs),
         out_shape=jax.ShapeDtypeStruct((q_dev, cands), jnp.float32),
-        in_specs=[whole()] * 4,
+        in_specs=[whole()] * 3,
         out_specs=whole(),
         name="final",
         compiler_params=pltpu.CompilerParams(vmem_limit_bytes=8 << 20),
-    )(cand_owner, cand_row, queries, returned)
+    )(place, queries, returned)
     return pq.transpose(0, 2, 1), rerank
 
 

time: 38 us -> 39.3 us (1.034)
  local copies, waits for them, and re-layouts: 2.96 us -> 4.33 us
    unnamed x14, local copies, waits for them, and re-layouts: 2.96 us -> 4.33 us
  transfers between devices with their start and end apart: 6 -> 6, of which waited for: 1 -> 1; matrix products, arithmetic and copies ran while one was open for 0% -> 0% of each run, Pallas kernels for 32% -> 31%
where the time goes in v4:
time: 39.3 us; the launch traced here: 38.8 us
  starting transfers between devices  16.1 us (41%)
  Pallas kernels  13.4 us (34%)
  local copies, waits for them, and re-layouts  4.33 us (11%)
  waiting for transfers between devices  4.25 us (11%)
  between operations  0.76 us (2%)
    pallas_call x1, Pallas kernels, per_device(): pl.pallas_call(lambda *refs: pq_kernel(q_dev, pieces, unroll, *refs), out...  9.45 us
    all_to_all x1, starting transfers between devices, per_device(): asked = lax.all_to_all(ids, AXES, split_axis=0, concat_axis=0, tiled=True)  7.16 us
    all_to_all x1, starting transfers between devices, per_device(): lax.all_to_all(rows, AXES, split_axis=0, concat_axis=0, tiled=True)  4.9 us
    unnamed x14, local copies, waits for them, and re-layouts  4.33 us
    all_to_all x1, waiting for transfers between devices, per_device(): asked = lax.all_to_all(ids, AXES, split_axis=0, concat_axis=0, tiled=True)  4.24 us
    ppermute x3, starting transfers between devices, per_device(): lax.ppermute(own, 'shard', [(i, i ^ k) for i in range(shards)])  3.56 us
    pallas_call x1, Pallas kernels, per_device(): pl.pallas_call(lambda *refs: ids_kernel(capacity, parts, *refs), out_shap...  1.53 us
    pallas_call x1, Pallas kernels, per_device(): pl.pallas_call(kernel, out_shape=jax.ShapeDtypeStruct((owners, SUB, piece...  1.12 us
  transfers between devices with their start and end apart: 6, of which 1 were waited for; matrix products, arithmetic and copies ran while one was open for 0% of the time, Pallas kernels for 31%

profile of v4, /device:TPU:13, one launch (start us, length us, event | category | flops | bytes accessed | tf_op | source)
XLA Modules:
  0.0 38.8 jit_solution(9492066129272484576)
XLA Ops:
  0.6 0.0 copy-start
  0.6 0.0 copy-start.4
  0.6 0.7 %copy-done.4 = s32[64,8]{0,1:T(8,128)S(1)} copy-done((s32[64,8]{0,1:T(8,128)S(1)}, s32[64,8]{0,1:T(8,128)}, u32[]{:S(2)}) %copy-start.4) | copy-done | bytes 2072
  1.3 0.0 copy-start.5
  1.3 0.7 %copy-done.5 = s32[8,16]{1,0:T(8,128)S(1)} copy-done((s32[8,16]{1,0:T(8,128)S(1)}, s32[8,16]{1,0:T(8,128)}, u32[]{:S(2)}) %copy-start.5) | copy-done | bytes 536
  2.0 0.0 copy-start.6
  2.0 0.7 %copy-done.6 = s32[8,16]{1,0:T(8,128)S(1)} copy-done((s32[8,16]{1,0:T(8,128)S(1)}, s32[8,16]{1,0:T(8,128)}, u32[]{:S(2)}) %copy-start.6) | copy-done | bytes 536
  2.7 0.3 groups.1
  3.0 0.0 copy-done
  3.0 0.0 copy-start.1
  3.0 1.4 %collective-permute-start.2 = (f32[8,768]{1,0:T(8,128)S(1)}, f32[8,768]{1,0:T(8,128)S(1)}, u32[]{:S(2)}, u32[]{:S(2)}) collective-permute-start(f32[8,768]{1,0:T(8,128)S(1)} %copy-done), channel_id=1, source_target_pairs={{0,6},{1,7},{2,4},{3,5},{4,2},{5,3},{6,0},{7,1},{8,14},{9,15},{10,... | collective-permute-start | bytes 73736 | tf_op jit(solution)/shard_map/ppermute | solution.py:369
  4.4 1.1 %collective-permute-start.1 = (f32[8,768]{1,0:T(8,128)S(1)}, f32[8,768]{1,0:T(8,128)S(1)}, u32[]{:S(2)}, u32[]{:S(2)}) collective-permute-start(f32[8,768]{1,0:T(8,128)S(1)} %copy-done), channel_id=1, source_target_pairs={{0,4},{1,5},{2,6},{3,7},{4,0},{5,1},{6,2},{7,3},{8,12},{9,13},{10,... | collective-permute-start | bytes 73736 | tf_op jit(solution)/shard_map/ppermute | solution.py:369
  5.5 1.1 %collective-permute-start = (f32[8,768]{1,0:T(8,128)S(1)}, f32[8,768]{1,0:T(8,128)S(1)}, u32[]{:S(2)}, u32[]{:S(2)}) collective-permute-start(f32[8,768]{1,0:T(8,128)S(1)} %copy-done), channel_id=1, source_target_pairs={{0,2},{1,3},{2,0},{3,1},{4,6},{5,7},{6,4},{7,5},{8,10},{9,11},{10,... | collective-permute-start | bytes 73736 | tf_op jit(solution)/shard_map/ppermute | solution.py:369
  6.6 1.5 %ids.1 = s32[32,1,128]{2,1,0:T(1,128)} custom-call(s32[8,16]{1,0:T(8,128)} %refs_0_.3, s32[8,16]{1,0:T(8,128)} %refs_1_.4), custom_call_target="tpu_custom_call" | custom-call | flops 1000000000 | bytes 6291456 | tf_op jit(solution)/shard_map/ids/pallas_call | solution.py:341
  8.1 7.2 %all-to-all-start = ((s32[32,1,128]{2,1,0:T(1,128)}), s32[32,1,128]{2,1,0:T(1,128)S(1)}, u32[]{:S(2)}, u32[]{:S(2)}) async-start(s32[32,1,128]{2,1,0:T(1,128)} %ids.1), calls=%async_computation | async-start | bytes 32768 | tf_op jit(solution)/shard_map/all_to_all | solution.py:364
  15.3 0.0 collective-permute-done.2.refs_3_
  15.3 0.0 collective-permute-done.1.refs_2_
  15.3 0.0 collective-permute-done.refs_1_
  15.4 0.5 %collective-permute-start.3 = (f32[32,768]{1,0:T(8,128)S(1)}, f32[32,768]{1,0:T(8,128)}, u32[]{:S(2)}, u32[]{:S(2)}) collective-permute-start(f32[32,768]{1,0:T(8,128)S(1)} %join.1.refs_3_.refs_4_.refs_5_.refs_6_), channel_id=1, source_target_pairs={{0,1},{1,0},{2,3},{3,2},{4,5},{5,4},{6,7},{7,6},{8,9},{9,8},{10,11... | collective-permute-start | bytes 294920 | tf_op jit(solution)/shard_map/ppermute | solution.py:406
  15.8 4.2 %all-to-all-done.ids_ref = s32[32,1,128]{2,1,0:T(1,128)S(1)} async-done(((s32[32,1,128]{2,1,0:T(1,128)}), s32[32,1,128]{2,1,0:T(1,128)S(1)}, u32[]{:S(2)}, u32[]{:S(2)}) %all-to-all-start) | async-done | bytes 16416 | tf_op jit(solution)/shard_map/all_to_all | solution.py:364
  20.1 0.0 copy-done.1
  20.1 1.1 %rows.1 = bf16[32,8,384]{2,1,0:T(8,128)(2,1)} custom-call(s32[32,1,128]{2,1,0:T(1,128)S(1)} %all-to-all-done.ids_ref, f32[1024,768]{1,0:T(8,128)S(1)} %copy-done.1), custom_call_target="tpu_custom_call" | custom-call | flops 1000000000 | bytes 4194304 | tf_op jit(solution)/shard_map/rows/pallas_call | solution.py:384
  21.2 4.9 %all-to-all-start.1 = ((bf16[32,8,384]{2,1,0:T(8,128)(2,1)}), bf16[32,8,384]{2,1,0:T(8,128)(2,1)S(1)}, u32[]{:S(2)}, u32[]{:S(2)}) async-start(bf16[32,8,384]{2,1,0:T(8,128)(2,1)} %rows.1), calls=%async_computation.1 | async-start | bytes 393216 | tf_op jit(solution)/shard_map/all_to_all | solution.py:394
  26.1 0.0 collective-permute-done.3.refs_7_.refs_8_.refs_9_.refs_10_
  26.1 0.0 copy-start.2
  26.1 1.1 %copy-done.2 = f32[96,256,8]{1,2,0:T(8,128)S(1)} copy-done((f32[96,256,8]{1,2,0:T(8,128)S(1)}, f32[96,256,8]{1,2,0:T(8,128)}, u32[]{:S(2)}) %copy-start.2) | copy-done | bytes 786456
  27.2 0.0 copy-start.3
  27.2 1.1 %copy-done.3 = s32[8,96,256]{2,1,0:T(8,128)S(1)} copy-done((s32[8,96,256]{2,1,0:T(8,128)S(1)}, s32[8,96,256]{2,1,0:T(8,128)}, u32[]{:S(2)}) %copy-start.3) | copy-done | bytes 786456
  28.4 9.5 %pq.1 = f32[8,64,256]{2,1,0:T(8,128)} custom-call(s32[8,128]{1,0:T(8,128)S(1)} %get-tuple-element.7.refs_0_, f32[768,256]{1,0:T(8,128)S(1)} %bitcast.5, s32[8,96,256]{2,1,0:T(8,128)S(1)} %copy-done.3, f32[32,768]{1,0:T(8,128)S(1)} %join.1.refs_3_.refs_4_.refs_5_.refs_6_, f32[32,768]{1,0:T(8,128)S(1)} %join.1.refs_3_.refs_4_.refs_5_.refs_6_, ...), custom_call_target="tpu_custom_call" | custom-call | flops 10000000000 | bytes 31457280 | tf_op jit(solution)/shard_map/pq/pallas_call | solution.py:415
  37.8 0.0 all-to-all-done.1.refs_2_
  37.9 1.0 %final.1 = f32[8,16]{1,0:T(8,128)} custom-call(s32[8,128]{1,0:T(8,128)S(1)} %get-tuple-element.9.refs_0_, f32[8,768]{1,0:T(8,128)S(1)} %copy-done, bf16[32,8,384]{2,1,0:T(8,128)(2,1)S(1)} %all-to-all-done.1.refs_2_), custom_call_target="tpu_custom_call" | custom-call | tf_op jit(solution)/shard_map/final/pallas_call | solution.py:442
  (1 shorter events, 0.0 us)
Async XLA Ops:
  0.6 2.4 %copy-start = (f32[8,768]{1,0:T(8,128)S(1)}, f32[8,768]{1,0:T(8,128)}, u32[]{:S(2)}) copy-start(f32[8,768]{1,0:T(8,128)} %refs_1_.5) | copy-start | bytes 73732
  0.6 0.7 %copy-start.4 = (s32[64,8]{0,1:T(8,128)S(1)}, s32[64,8]{0,1:T(8,128)}, u32[]{:S(2)}) copy-start(s32[64,8]{0,1:T(8,128)} %param.10) | copy-start | bytes 6148
  1.3 0.7 %copy-start.5 = (s32[8,16]{1,0:T(8,128)S(1)}, s32[8,16]{1,0:T(8,128)}, u32[]{:S(2)}) copy-start(s32[8,16]{1,0:T(8,128)} %refs_0_.3) | copy-start | bytes 1540
  2.0 0.7 %copy-start.6 = (s32[8,16]{1,0:T(8,128)S(1)}, s32[8,16]{1,0:T(8,128)}, u32[]{:S(2)}) copy-start(s32[8,16]{1,0:T(8,128)} %refs_1_.4) | copy-start | bytes 1540
  3.0 17.0 %copy-start.1 = (f32[1024,768]{1,0:T(8,128)S(1)}, f32[1024,768]{1,0:T(8,128)}, u32[]{:S(2)}) copy-start(f32[1024,768]{1,0:T(8,128)} %vectors_ref.1) | copy-start | bytes 9437188
  3.0 12.3 %collective-permute-start.2 = (f32[8,768]{1,0:T(8,128)S(1)}, f32[8,768]{1,0:T(8,128)S(1)}, u32[]{:S(2)}, u32[]{:S(2)}) collective-permute-start(f32[8,768]{1,0:T(8,128)S(1)} %copy-done), channel_id=1, source_target_pairs={{0,6},{1,7},{2,4},{3,5},{4,2},{5,3},{6,0},{7,1},{8,14},{9,15},{10,... | collective-permute-start | bytes 73736 | tf_op jit(solution)/shard_map/ppermute | solution.py:369
  4.4 10.9 %collective-permute-start.1 = (f32[8,768]{1,0:T(8,128)S(1)}, f32[8,768]{1,0:T(8,128)S(1)}, u32[]{:S(2)}, u32[]{:S(2)}) collective-permute-start(f32[8,768]{1,0:T(8,128)S(1)} %copy-done), channel_id=1, source_target_pairs={{0,4},{1,5},{2,6},{3,7},{4,0},{5,1},{6,2},{7,3},{8,12},{9,13},{10,... | collective-permute-start | bytes 73736 | tf_op jit(solution)/shard_map/ppermute | solution.py:369
  5.5 9.8 %collective-permute-start = (f32[8,768]{1,0:T(8,128)S(1)}, f32[8,768]{1,0:T(8,128)S(1)}, u32[]{:S(2)}, u32[]{:S(2)}) collective-permute-start(f32[8,768]{1,0:T(8,128)S(1)} %copy-done), channel_id=1, source_target_pairs={{0,2},{1,3},{2,0},{3,1},{4,6},{5,7},{6,4},{7,5},{8,10},{9,11},{10,... | collective-permute-start | bytes 73736 | tf_op jit(solution)/shard_map/ppermute | solution.py:369
  8.1 11.9 %all-to-all-start = ((s32[32,1,128]{2,1,0:T(1,128)}), s32[32,1,128]{2,1,0:T(1,128)S(1)}, u32[]{:S(2)}, u32[]{:S(2)}) async-start(s32[32,1,128]{2,1,0:T(1,128)} %ids.1), calls=%async_computation | async-start | bytes 32768 | tf_op jit(solution)/shard_map/all_to_all | solution.py:364
  15.4 10.7 %collective-permute-start.3 = (f32[32,768]{1,0:T(8,128)S(1)}, f32[32,768]{1,0:T(8,128)}, u32[]{:S(2)}, u32[]{:S(2)}) collective-permute-start(f32[32,768]{1,0:T(8,128)S(1)} %join.1.refs_3_.refs_4_.refs_5_.refs_6_), channel_id=1, source_target_pairs={{0,1},{1,0},{2,3},{3,2},{4,5},{5,4},{6,7},{7,6},{8,9},{9,8},{10,11... | collective-permute-start | bytes 294920 | tf_op jit(solution)/shard_map/ppermute | solution.py:406
  21.2 16.7 %all-to-all-start.1 = ((bf16[32,8,384]{2,1,0:T(8,128)(2,1)}), bf16[32,8,384]{2,1,0:T(8,128)(2,1)S(1)}, u32[]{:S(2)}, u32[]{:S(2)}) async-start(bf16[32,8,384]{2,1,0:T(8,128)(2,1)} %rows.1), calls=%async_computation.1 | async-start | bytes 393216 | tf_op jit(solution)/shard_map/all_to_all | solution.py:394
  26.1 1.1 %copy-start.2 = (f32[96,256,8]{1,2,0:T(8,128)S(1)}, f32[96,256,8]{1,2,0:T(8,128)}, u32[]{:S(2)}) copy-start(f32[96,256,8]{1,2,0:T(8,128)} %param.8) | copy-start | bytes 2359300
  27.2 1.1 %copy-start.3 = (s32[8,96,256]{2,1,0:T(8,128)S(1)}, s32[8,96,256]{2,1,0:T(8,128)}, u32[]{:S(2)}) copy-start(s32[8,96,256]{2,1,0:T(8,128)} %refs_2_.3) | copy-start | bytes 2359300
